TPU v7x, 32 devices: a whole 2x2x4 slice. The times are simulated.
32 devices in a mesh: dp: 16 (over z, x, core), tensor: 2 (over y).
Axes of the slice: x: 2, y: 2, z: 4, core: 2. Of those that a mesh axis runs over, the one named last changes fastest.
Arguments:
- tokens: bfloat16 [19712, 512], P('dp'), may hold values from -6 to 6
- lengths: int32 [256], P('dp'), may hold values from 5 to 77, as said below
- qkv_weight: bfloat16 [3, 512, 512], P(None, None, 'tensor'), may hold values from -0.375 to 0.375
- qv_bias: bfloat16 [2, 512], P(None, 'tensor'), may hold values from -3 to 3
- out_weight: bfloat16 [512, 512], P('tensor'), may hold values from -0.75 to 0.75
- out_bias: bfloat16 [512], replicated, may hold values from -3 to 3
- up_weight: bfloat16 [512, 2048], P(None, 'tensor'), may hold values from -0.25 to 0.25
- up_bias: bfloat16 [2048], P('tensor'), may hold values from -3 to 3
- down_weight: bfloat16 [2048, 512], P('tensor'), may hold values from -0.1875 to 0.1875
- down_bias: bfloat16 [512], replicated, may hold values from -3 to 3
- norm_gain: bfloat16 [2, 512], replicated, may hold values from 0.099609375 to 1.8984375
- norm_shift: bfloat16 [2, 512], replicated, may hold values from -3 to 3
- cotangent: bfloat16 [19712, 512], P('dp'), may hold values from -6 to 6
Outputs:
- layer_out: bfloat16 [19712, 512], P(('dp', 'tensor'))
- input_grad: float32 [19712, 512], P(('dp', 'tensor'))
- qkv_grad: float32 [3, 512, 512], P(None, None, 'tensor')
- qv_bias_grad: float32 [2, 512], P(None, 'tensor')
- out_weight_grad: float32 [512, 512], P('tensor')
- out_bias_grad: float32 [512], replicated
- up_weight_grad: float32 [512, 2048], P(None, 'tensor')
- up_bias_grad: float32 [2048], P('tensor')
- down_weight_grad: float32 [2048, 512], P('tensor')
- down_bias_grad: float32 [512], replicated
- norm_gain_grad: float32 [2, 512], replicated
- norm_shift_grad: float32 [2, 512], replicated
Inputs may be any that keep to these rules, and one draw needn't show every extreme that they name: `lengths`: in each aligned block of 16 captions one caption has exactly 77 tokens.
All inputs are finite; a program needn't handle non-finite values.
Results may differ from a plain program's by a relative error of at most 0.02.
Values may be sent and summed in bfloat16 or wider, within the bound.
A program may use at most 128 MiB of HBM per device.

v0:
```python
import jax
import jax.numpy as jnp
from jax import lax
from jax.sharding import PartitionSpec as P

HD = 64


EPSILON = 1e-05


def matmul_plain(left, right):
    return jnp.dot(left, right, preferred_element_type=jnp.float32)


def contract_rows(left, right):
    return lax.dot_general(
        left, right, (((0,), (0,)), ((), ())), preferred_element_type=jnp.float32
    )


def contract_cols(left, right):
    return lax.dot_general(
        left, right, (((1,), (1,)), ((), ())), preferred_element_type=jnp.float32
    )


def norm_stats(values):
    center = values - jnp.mean(values, axis=-1, keepdims=True)
    inv_std = lax.rsqrt(jnp.mean(center * center, axis=-1, keepdims=True) + EPSILON)
    return (center * inv_std, inv_std)


def norm_back(upstream, normed, inv_std, gain_vec):
    scaled = upstream * gain_vec
    inner_mean = jnp.mean(scaled * normed, axis=-1, keepdims=True)
    result = inv_std * (scaled - jnp.mean(scaled, axis=-1, keepdims=True) - normed * inner_mean)
    return (result, jnp.sum(upstream * normed, axis=0), jnp.sum(upstream, axis=0))


def row_slice(values, row_start, share_rows):
    return lax.dynamic_slice_in_dim(values, row_start, share_rows, 0)


def shards(
    tokens,
    lengths,
    qkv_weight,
    qv_bias,
    out_weight,
    out_bias,
    up_weight,
    up_bias,
    down_weight,
    down_bias,
    norm_gain,
    norm_shift,
    cotangent,
):
    tensor_count = lax.axis_size("tensor")
    tensor_index = lax.axis_index("tensor")
    share_rows = tokens.shape[0] // tensor_count
    row_start = tensor_index * share_rows
    gains = norm_gain.astype(jnp.float32)
    shifts = norm_shift.astype(jnp.float32)
    total_rows = tokens.shape[0]
    count = lengths.shape[0]
    slots = total_rows // count
    local_width = qkv_weight.shape[2]
    local_heads = local_width // HD
    score_scale = HD ** (-0.5)
    qv_float = qv_bias.astype(jnp.float32)
    token_f = tokens.astype(jnp.float32)
    normed_one, inv_one = norm_stats(token_f)
    first_in = (normed_one * gains[0] + shifts[0]).astype(jnp.bfloat16)
    queries = (matmul_plain(first_in, qkv_weight[0]) + qv_float[0]).astype(jnp.bfloat16)
    keys_all = matmul_plain(first_in, qkv_weight[1]).astype(jnp.bfloat16)
    values_all = (matmul_plain(first_in, qkv_weight[2]) + qv_float[1]).astype(jnp.bfloat16)
    shape4 = (count, slots, local_heads, HD)
    query_four = queries.reshape(shape4)
    key_four = keys_all.reshape(shape4)
    value_four = values_all.reshape(shape4)
    position = jnp.arange(slots)
    allowed = (position[None, :] <= position[:, None])[None, :, :] & (
        position[None, None, :] < lengths[:, None, None]
    )
    allowed = allowed[:, None, :, :]

    def masked_scores():
        raw = jnp.einsum(
            "cihd,cjhd->chij", query_four, key_four, preferred_element_type=jnp.float32
        )
        return jnp.where(allowed, raw * score_scale, -1e30)

    scores = masked_scores()
    row_max = jnp.max(scores, axis=-1, keepdims=True)
    log_total = row_max + jnp.log(jnp.sum(jnp.exp(scores - row_max), axis=-1, keepdims=True))
    probs_low = jnp.exp(scores - log_total).astype(jnp.bfloat16)
    context = jnp.einsum(
        "chij,cjhd->cihd", probs_low, value_four, preferred_element_type=jnp.float32
    )
    context = context.reshape(total_rows, local_width).astype(jnp.bfloat16)
    attn_part = matmul_plain(context, out_weight)
    attn_out = lax.psum(attn_part, "tensor") + out_bias.astype(jnp.float32)
    hidden_res = token_f + attn_out
    normed_two, inv_two = norm_stats(hidden_res)
    second_in = (normed_two * gains[1] + shifts[1]).astype(jnp.bfloat16)
    upper = matmul_plain(second_in, up_weight) + up_bias.astype(jnp.float32)
    sigma = jax.nn.sigmoid(1.702 * upper)
    hidden = (upper * sigma).astype(jnp.bfloat16)
    mlp_part = matmul_plain(hidden, down_weight)
    result_rows = (
        hidden_res
        + lax.psum(mlp_part.astype(jnp.bfloat16), "tensor").astype(jnp.float32)
        + down_bias.astype(jnp.float32)
    )
    layer_out = row_slice(result_rows, row_start, share_rows).astype(jnp.bfloat16)
    grad_f = cotangent.astype(jnp.float32)
    down_grad = contract_rows(hidden, cotangent)
    down_bias_grad = jnp.sum(grad_f, axis=0)
    hidden_grad = contract_cols(cotangent, down_weight)
    upper_grad = (hidden_grad * (sigma + 1.702 * upper * sigma * (1.0 - sigma))).astype(
        jnp.bfloat16
    )
    up_grad = contract_rows(second_in, upper_grad)
    up_bias_grad = jnp.sum(upper_grad.astype(jnp.float32), axis=0)
    second_part = contract_cols(upper_grad, up_weight)
    second_grad = lax.psum(second_part, "tensor")
    residual_back, gain_two, shift_two = norm_back(second_grad, normed_two, inv_two, gains[1])
    residual_full = grad_f + residual_back
    branch_grad = residual_full.astype(jnp.bfloat16)
    out_bias_grad = jnp.sum(branch_grad.astype(jnp.float32), axis=0)
    out_grad = contract_rows(context, branch_grad)
    context_grad = contract_cols(branch_grad, out_weight).astype(jnp.bfloat16).reshape(shape4)
    probs = jnp.exp(masked_scores() - log_total)
    probs_low = probs.astype(jnp.bfloat16)
    value_grad = jnp.einsum(
        "chij,cihd->cjhd", probs_low, context_grad, preferred_element_type=jnp.float32
    )
    prob_grad = jnp.einsum(
        "cihd,cjhd->chij", context_grad, value_four, preferred_element_type=jnp.float32
    )
    score_grad = probs * (prob_grad - jnp.sum(prob_grad * probs, axis=-1, keepdims=True))
    score_grad = score_grad.astype(jnp.bfloat16)
    query_grad = (
        jnp.einsum("chij,cjhd->cihd", score_grad, key_four, preferred_element_type=jnp.float32)
        * score_scale
    )
    key_grad = (
        jnp.einsum("chij,cihd->cjhd", score_grad, query_four, preferred_element_type=jnp.float32)
        * score_scale
    )
    query_grad = query_grad.reshape(total_rows, local_width).astype(jnp.bfloat16)
    key_grad = key_grad.reshape(total_rows, local_width).astype(jnp.bfloat16)
    value_grad = value_grad.reshape(total_rows, local_width).astype(jnp.bfloat16)
    qkv_grad = jnp.stack(
        [
            contract_rows(first_in, query_grad),
            contract_rows(first_in, key_grad),
            contract_rows(first_in, value_grad),
        ]
    )
    qv_bias_grad = jnp.stack(
        [
            jnp.sum(query_grad.astype(jnp.float32), axis=0),
            jnp.sum(value_grad.astype(jnp.float32), axis=0),
        ]
    )
    first_part = (
        contract_cols(query_grad, qkv_weight[0])
        + contract_cols(key_grad, qkv_weight[1])
        + contract_cols(value_grad, qkv_weight[2])
    )
    first_grad = lax.psum(first_part.astype(jnp.bfloat16), "tensor").astype(jnp.float32)
    input_back, gain_one, shift_one = norm_back(first_grad, normed_one, inv_one, gains[0])
    input_grad = row_slice(residual_full + input_back, row_start, share_rows)
    gain_grads = jnp.stack([gain_one, gain_two])
    shift_grads = jnp.stack([shift_one, shift_two])
    summed = (
        lax.psum(qkv_grad.astype(jnp.bfloat16), "dp").astype(jnp.float32),
        lax.psum(qv_bias_grad.astype(jnp.bfloat16), "dp").astype(jnp.float32),
        lax.psum(out_grad.astype(jnp.bfloat16), "dp").astype(jnp.float32),
        lax.psum(out_bias_grad.astype(jnp.bfloat16), "dp").astype(jnp.float32),
        lax.psum(up_grad.astype(jnp.bfloat16), "dp").astype(jnp.float32),
        lax.psum(up_bias_grad.astype(jnp.bfloat16), "dp").astype(jnp.float32),
        lax.psum(down_grad.astype(jnp.bfloat16), "dp").astype(jnp.float32),
        lax.psum(down_bias_grad.astype(jnp.bfloat16), "dp").astype(jnp.float32),
        lax.psum(gain_grads.astype(jnp.bfloat16), "dp").astype(jnp.float32),
        lax.psum(shift_grads.astype(jnp.bfloat16), "dp").astype(jnp.float32),
    )
    return (
        layer_out,
        input_grad,
        summed[0],
        summed[1],
        summed[2],
        summed[3],
        summed[4],
        summed[5],
        summed[6],
        summed[7],
        summed[8],
        summed[9],
    )


def solution(mesh):
    return jax.shard_map(
        shards,
        mesh=mesh,
        in_specs=(
            P("dp", None),
            P("dp"),
            P(None, None, "tensor"),
            P(None, "tensor"),
            P("tensor", None),
            P(),
            P(None, "tensor"),
            P("tensor"),
            P("tensor", None),
            P(),
            P(),
            P(),
            P("dp", None),
        ),
        out_specs=(
            P(("dp", "tensor"), None),
            P(("dp", "tensor"), None),
            P(None, None, "tensor"),
            P(None, "tensor"),
            P("tensor", None),
            P(),
            P(None, "tensor"),
            P("tensor"),
            P("tensor", None),
            P(),
            P(),
            P(),
        ),
        check_vma=False,
    )
```

profile of v0, /device:TPU:0, one launch (start us, length us, event | category | flops | bytes accessed | tf_op | source)
XLA Modules:
  0.0 479.0 jit_solution(13665965624036335371)
XLA Ops:
  18.9 3.0 reshape.142
  21.9 3.4 copy.42
  26.8 2.7 copy.40
  29.5 3.3 reshape.144
  32.8 3.4 copy.41
  45.0 3.0 fusion.46
  48.3 74.8 %all-reduce.8.cloned.1.call-done = f32[1232,512]{1,0:T(8,128)} async-done(((f32[1232,512]{1,0:T(8,128)}), f32[1232,512]{1,0:T(8,128)}) %all-reduce.8.cloned.1.call-update) | async-done | bytes 2523152 | tf_op jit(solution)/shard_map/psum | solution.py:104
  126.0 3.8 multiply_convert_fusion.1
  129.8 3.8 fusion.45
  135.1 3.0 fusion.47
  138.1 4.7 convolution_convert_fusion.5
  142.9 2.8 convolution_convert_fusion.6
  145.7 64.7 %all-reduce.10.cloned.1.call-done = f32[1232,512]{1,0:T(8,128)} async-done(((f32[1232,512]{1,0:T(8,128)}), f32[1232,512]{1,0:T(8,128)}) %all-reduce.10.cloned.1.call-update) | async-done | bytes 2523152 | tf_op jit(solution)/shard_map/psum | solution.py:128
  210.4 3.4 multiply_reduce_fusion.1
  219.5 3.5 copy.46
  223.1 3.8 fusion.43
  233.1 2.6 fusion.18
  237.7 2.6 fusion.17
  246.5 4.5 convolution_convert_fusion
  254.2 96.2 %all-reduce.12.cloned.1.call-done = (bf16[3,512,256]{2,1,0:T(8,128)(2,1)}, bf16[256,512]{1,0:T(8,128)(2,1)}, bf16[512,1024]{1,0:T(8,128)(2,1)}, bf16[1024,512]{1,0:T(8,128)(2,1)}) async-done(((bf16[3,512,256]{2,1,0:T(8,128)(2,1)}, bf16[256,512]{1,0:T(8,128)(2,1)}, bf16[512,1024]{1,0:T(8,128)(2,1)}, bf16[1024,512]{1,0:T(8,128)(2,1)}), (bf16[3,512,256]{2,1,0:T(8,128)(2,1)}, bf16[256,512]{1,0:T(8,128)(2,1)}, ...) | async-done | bytes 3145744 | tf_op jit(solution)/shard_map/psum | solution.py:180
  357.9 66.4 %all-reduce.14.cloned.1.call-done = (bf16[1232,512]{1,0:T(8,128)(2,1)}, bf16[1232,512]{1,0:T(8,128)(2,1)}) async-done(((bf16[1232,512]{1,0:T(8,128)(2,1)}, bf16[1232,512]{1,0:T(8,128)(2,1)}), (bf16[1232,512]{1,0:T(8,128)(2,1)}, bf16[1232,512]{1,0:T(8,128)(2,1)})) %all-reduce.14.cloned.1.call-update) | async-done | bytes 2523152 | tf_op jit(solution)/shard_map/psum | solution.py:114
  424.4 5.2 %fusion.6 = (bf16[512]{0:T(512)(128)(2,1)S(1)}, f32[1232]{0:T(1024)S(1)}, f32[1232]{0:T(1024)S(1)}, f32[1232,512]{1,0:T(8,128)}, f32[1232,512]{1,0:T(8,128)}) fusion(bf16[1232,512]{1,0:T(8,128)(2,1)} %get-tuple-element.30, f32[1232]{0:T(1024)S(1)} %copy-done.30, f32[1232]{0:T(1024)S(1)} %copy-done.28, bf16[1232,512]{1,0:T(8,128)(2,1)S(1)} %copy-done.7, ...), kind=kLoop, calls=%fused_computation.26 | loop fusion | flops 6304864 | bytes 7592192 | tf_op jit(solution)/shard_map/reduce_sum | solution.py:38
  429.9 34.1 %all-reduce = (bf16[2,256]{1,0:T(2,128)(2,1)S(1)}, bf16[512]{0:T(512)(128)(2,1)S(1)}, bf16[1024]{0:T(1024)(128)(2,1)S(1)}, bf16[512]{0:T(512)(128)(2,1)S(1)}, bf...) all-reduce(bf16[2,256]{1,0:T(2,128)(2,1)S(1)} %pad_maximum_fusion.3, ...), channel_id=1, replica_groups=mesh['dp'=16,'tensor'=2] {'dp'}, use_global_device_ids=true, to_apply=%region_18.19 | all-reduce | flops 4608 | bytes 18432 | tf_op jit(solution)/shard_map/psum | solution.py:181
  467.7 4.3 dynamic-slice_add_fusion
  (175 shorter events, 61.1 us)
Async XLA Ops:
  7.2 118.6 %copy-start = (bf16[512,1024]{1,0:T(8,128)(2,1)S(1)}, bf16[512,1024]{1,0:T(8,128)(2,1)}, u32[]{:S(2)}) copy-start(bf16[512,1024]{1,0:T(8,128)(2,1)} %param.19) | copy-start | bytes 3145732
  7.2 7.9 %copy-start.6 = (bf16[1232,512]{1,0:T(8,128)(2,1)S(1)}, bf16[1232,512]{1,0:T(8,128)(2,1)}, u32[]{:S(2)}) copy-start(bf16[1232,512]{1,0:T(8,128)(2,1)} %param.13) | copy-start | bytes 3784708
  7.2 115.9 %all-reduce.8.cloned.1.call-start = ((), (), s32[]{:S(2)}) async-start(), calls=%async_computation | async-start | bytes 5046272 | tf_op jit(solution)/shard_map/psum | solution.py:104
  10.2 5.4 %copy-start.31 = (f32[1,512]{1,0:T(1,128)}, f32[1,512]{1,0:T(1,128)S(1)}, u32[]{:S(2)}) copy-start(f32[1,512]{1,0:T(1,128)S(1)} %get-tuple-element.39) | copy-start | bytes 6148
  11.6 4.1 copy-start.24
  29.5 8.9 %copy-start.10 = (bf16[16,77,4,64]{1,3,2,0:T(8,128)(2,1)}, bf16[16,77,4,64]{1,3,2,0:T(8,128)(2,1)S(1)}, u32[]{:S(2)}) copy-start(bf16[16,77,4,64]{1,3,2,0:T(8,128)(2,1)S(1)} %copy.40) | copy-start | bytes 1892356
  48.0 162.4 %all-reduce.10.cloned.1.call-start = ((), (), s32[]{:S(2)}) async-start(), calls=%async_computation.1 | async-start | bytes 5046272 | tf_op jit(solution)/shard_map/psum | solution.py:128
  125.2 4.6 copy-start.4
  138.1 212.3 %all-reduce.12.cloned.1.call-start = ((), (), s32[]{:S(2)}) async-start(), calls=%async_computation.2 | async-start | bytes 6291456 | tf_op jit(solution)/shard_map/psum | solution.py:180
  138.1 4.8 copy-start.5
  138.1 4.7 copy-start.46
  217.9 5.1 %copy-start.3 = (f32[16,4,77,77]{2,3,1,0:T(8,128)S(1)}, f32[16,4,77,77]{2,3,1,0:T(8,128)}, u32[]{:S(2)}) copy-start(f32[16,4,77,77]{2,3,1,0:T(8,128)} %copy-done.2) | copy-start | bytes 4553476
  246.1 4.8 %copy-start.25 = (bf16[3,512,256]{2,1,0:T(8,128)(2,1)S(1)}, bf16[3,512,256]{2,1,0:T(8,128)(2,1)}, u32[]{:S(2)}) copy-start(bf16[3,512,256]{2,1,0:T(8,128)(2,1)} %param.15) | copy-start | bytes 2359300
  246.2 178.2 %all-reduce.14.cloned.1.call-start = ((), (), s32[]{:S(2)}) async-start(), calls=%async_computation.3 | async-start | bytes 5046272 | tf_op jit(solution)/shard_map/psum | solution.py:114
  350.4 4.4 copy-start.21
  352.2 4.1 copy-start.20
  354.7 69.6 %copy-start.7 = (bf16[1232,512]{1,0:T(8,128)(2,1)S(1)}, bf16[1232,512]{1,0:T(8,128)(2,1)}, u32[]{:S(2)}) copy-start(bf16[1232,512]{1,0:T(8,128)(2,1)} %param.13) | copy-start | bytes 3784708
  354.8 69.6 %copy-start.28 = (f32[1232]{0:T(1024)S(1)}, f32[1232]{0:T(1024)}, u32[]{:S(2)}) copy-start(f32[1232]{0:T(1024)} %copy-done.27) | copy-start | bytes 14788
  354.8 69.6 %copy-start.32 = (f32[1,512]{1,0:T(1,128)S(1)}, f32[1,512]{1,0:T(1,128)}, u32[]{:S(2)}) copy-start(f32[1,512]{1,0:T(1,128)} %copy-done.31) | copy-start | bytes 6148
  424.3 5.3 %copy-start.15 = (bf16[1232,512]{1,0:T(8,128)(2,1)S(1)}, bf16[1232,512]{1,0:T(8,128)(2,1)}, u32[]{:S(2)}) copy-start(bf16[1232,512]{1,0:T(8,128)(2,1)} %get-tuple-element.30) | copy-start | bytes 3784708
  424.3 5.5 %copy-start.36 = (bf16[512]{0:T(512)(128)(2,1)S(1)}, bf16[512]{0:T(512)(128)(2,1)}, u32[]{:S(2)}) copy-start(bf16[512]{0:T(512)(128)(2,1)} %get-tuple-element.31) | copy-start | bytes 3076
  424.3 5.5 %copy-start.37 = (bf16[512]{0:T(512)(128)(2,1)S(1)}, bf16[512]{0:T(512)(128)(2,1)}, u32[]{:S(2)}) copy-start(bf16[512]{0:T(512)(128)(2,1)} %get-tuple-element.37) | copy-start | bytes 3076
  424.3 5.5 %copy-start.39 = (bf16[1024]{0:T(1024)(128)(2,1)S(1)}, bf16[1024]{0:T(1024)(128)(2,1)}, u32[]{:S(2)}) copy-start(bf16[1024]{0:T(1024)(128)(2,1)} %get-tuple-element.54) | copy-start | bytes 6148
  467.7 4.3 copy-start.1
  (27 other events, 65.1 us)
Sparse Core Ops, SparseCore 0:
  48.1 74.8 all-reduce.7
  138.2 72.1 all-reduce.9
  246.3 104.0 all-reduce.11
  353.1 71.1 all-reduce.13
where the time goes:
time: 488 us; the launch traced here: 479 us
  waiting for transfers between devices  302 us (62%)
  matrix products  49.8 us (10%)
  local copies, waits for them, and re-layouts  39.9 us (8%)
  other arithmetic  37.6 us (8%)
  blocking collectives  34.1 us (7%)
  between operations  14.9 us (3%)
    psum x1, waiting for transfers between devices, shards(): lax.psum(qkv_grad.astype(jnp.bfloat16), 'dp').astype(jnp.float32)  96.2 us
    psum x1, waiting for transfers between devices, shards(): attn_out = lax.psum(attn_part, 'tensor') + out_bias.astype(jnp.float32)  74.8 us
    psum x1, waiting for transfers between devices, shards(): lax.psum(mlp_part.astype(jnp.bfloat16), 'tensor').astype(jnp.float32)  66.4 us
    psum x1, waiting for transfers between devices, shards(): second_grad = lax.psum(second_part, 'tensor')  64.7 us
    psum x1, blocking collectives, shards(): lax.psum(qv_bias_grad.astype(jnp.bfloat16), 'dp').astype(jnp.float32)  34.1 us
    dot_general x6, matrix products, contract_rows(): lax.dot_general(left, right, (((0,), (0,)), ((), ())), preferred_element_...  16.2 us
    dot_general x6, matrix products, matmul_plain(): return jnp.dot(left, right, preferred_element_type=jnp.float32)  14.4 us
    dot_general x6, matrix products, contract_cols(): lax.dot_general(left, right, (((1,), (1,)), ((), ())), preferred_element_...  10.1 us
  transfers between devices with their start and end apart: 4, of which 4 were waited for; matrix products, arithmetic and copies ran while one was open for 5% of the time, Pallas kernels for 0%

commit v1 on v0

--- a/solution.py
+++ b/solution.py
@@ -1,12 +1,761 @@
+import functools
+
 import jax
 import jax.numpy as jnp
 from jax import lax
+from jax.experimental import pallas as pl
+from jax.experimental.pallas import tpu as pltpu
 from jax.sharding import PartitionSpec as P
 
 HD = 64
-
-
 EPSILON = 1e-05
+F32 = jnp.float32
+BF16 = jnp.bfloat16
+LOG2E = 1.4426950408889634
+UNITS = 12
+MESH = pl.DeviceIdType.MESH
+
+
+def nn(left, right):
+    return lax.dot_general(left, right, (((1,), (0,)), ((), ())), preferred_element_type=F32)
+
+
+def nt(left, right):
+    return lax.dot_general(left, right, (((1,), (1,)), ((), ())), preferred_element_type=F32)
+
+
+def tn(left, right):
+    return lax.dot_general(left, right, (((0,), (0,)), ((), ())), preferred_element_type=F32)
+
+
+def loop(count, body):
+    lax.fori_loop(0, count, lambda i, c: (body(i), c)[1], 0)
+
+
+def norm(rows):
+    center = rows - jnp.mean(rows, axis=-1, keepdims=True)
+    inv = lax.rsqrt(jnp.mean(center * center, axis=-1, keepdims=True) + EPSILON)
+    return center * inv, inv
+
+
+def norm_back(grad, normed, inv, gain):
+    t = grad * gain
+    inner = jnp.mean(t * normed, axis=-1, keepdims=True)
+    return inv * (t - jnp.mean(t, axis=-1, keepdims=True) - normed * inner)
+
+
+def colsum(x):
+    return jnp.sum(x, axis=0, keepdims=True)
+
+
+class Layer:
+    def __init__(self, caps, slots, pad, refs):
+        self.caps, self.slots, self.pad = caps, slots, pad
+        self.rows = caps * pad
+        self.__dict__.update(refs)
+
+    def head_mask(self, h, rows):
+        lane = lax.broadcasted_iota(jnp.int32, (rows, 256), 1)
+        return (lane >= h * HD) & (lane < (h + 1) * HD)
+
+    def stack(self, block):
+        parts = []
+        for h in range(4):
+            parts.append(jnp.where(self.head_mask(h, self.pad), block, jnp.zeros_like(block)))
+        return jnp.concatenate(parts, axis=0)
+
+    def unstack(self, block):
+        out = None
+        for h in range(4):
+            part = block[h * self.pad : (h + 1) * self.pad]
+            out = part if out is None else jnp.where(self.head_mask(h, self.pad), part, out)
+        return out
+
+    def widen(self, src, base, dst):
+        total = src.shape[0]
+        tile = self.slots * 2 if total % (self.slots * 2) == 0 else self.slots
+        tile = 176 if total % 176 == 0 else total
+        def conv(i):
+            r = pl.ds(pl.multiple_of(i * tile, 16), tile)
+            self.stage[r, :] = src[r, :].astype(F32)
+        loop(total // tile, conv)
+        self.stage[total : total + 16, :] = jnp.zeros((16, self.stage.shape[1]), F32)
+        for c in range(self.caps):
+            off = c * self.slots
+            low = off // 8 * 8
+            v = self.stage[pl.ds(pl.multiple_of(base + low, 8), self.pad + 8), :]
+            v = v[off - low : off - low + self.pad]
+            row = lax.broadcasted_iota(jnp.int32, v.shape, 0)
+            v = jnp.where(row < self.slots, v, 0.0)
+            dst[c * self.pad : (c + 1) * self.pad, :] = v.astype(BF16)
+
+    def crows(self, c):
+        return pl.ds(pl.multiple_of(c * self.pad, self.pad), self.pad)
+
+    def norm_one(self):
+        gain, shift = self.gains[0:1, :].astype(F32), self.shifts[0:1, :].astype(F32)
+        def cap(c):
+            r = self.crows(c)
+            n, inv = norm(self.xs[r, :].astype(F32))
+            self.n1[r, :] = n
+            self.r1[r, :] = jnp.broadcast_to(inv, (self.pad, 128))
+            self.a1[r, :] = (n * gain + shift).astype(BF16)
+        loop(self.caps, cap)
+
+    def qkv(self, i):
+        s, j = i // 3, lax.rem(i, 3)
+        out = nn(self.a1[...], self.w[s * UNITS + j]) + self.bias_qkv[i]
+        self.pqkv[i] = out.astype(BF16)
+
+    def attention(self, i):
+        s, c = i // self.caps, lax.rem(i, self.caps)
+        r = self.crows(c)
+        q = self.pqkv[s * 3, r, :]
+        km = self.stack(self.pqkv[s * 3 + 1, r, :])
+        vm = self.stack(self.pqkv[s * 3 + 2, r, :])
+        st = nt(km, q)
+        length = self.lengths[self.cap_base + c]
+        jj = lax.broadcasted_iota(jnp.int32, (self.pad, self.pad), 0)
+        ii = lax.broadcasted_iota(jnp.int32, (self.pad, self.pad), 1)
+        allowed = (jj <= ii) & (jj < length)
+        blocks = []
+        for h in range(4):
+            blk = jnp.where(allowed, st[h * self.pad : (h + 1) * self.pad], -1e30)
+            top = jnp.max(blk, axis=0, keepdims=True)
+            e = jnp.exp2((blk - top) * (HD**-0.5 * LOG2E))
+            blocks.append(e * (1.0 / jnp.sum(e, axis=0, keepdims=True)))
+        p = jnp.concatenate(blocks, axis=0)
+        self.probs[i] = p
+        self.ctx[s, r, :] = tn(p.astype(BF16), vm).astype(BF16)
+
+    def attention_back(self, i):
+        s, c = i // self.caps, lax.rem(i, self.caps)
+        r = self.crows(c)
+        q = self.pqkv[s * 3, r, :]
+        k = self.pqkv[s * 3 + 1, r, :]
+        v = self.pqkv[s * 3 + 2, r, :]
+        d = self.dctx[s, r, :]
+        p = self.probs[i]
+        self.dqkv[s * 3 + 2, r, :] = self.unstack(nn(p.astype(BF16), d)).astype(BF16)
+        dp = nt(self.stack(v), d)
+        blocks = []
+        for h in range(4):
+            rr = slice(h * self.pad, (h + 1) * self.pad)
+            blocks.append(p[rr] * (dp[rr] - jnp.sum(dp[rr] * p[rr], axis=0, keepdims=True)))
+        ds = jnp.concatenate(blocks, axis=0).astype(BF16)
+        self.dqkv[s * 3 + 1, r, :] = (self.unstack(nn(ds, q)) * HD**-0.5).astype(BF16)
+        self.dqkv[s * 3, r, :] = (tn(ds, self.stack(k)) * HD**-0.5).astype(BF16)
+
+    def project(self, i):
+        tile = self.rows // 4
+        r = pl.ds(pl.multiple_of(i * tile, 16), tile)
+        gain, shift = self.gains[1:2, :].astype(F32), self.shifts[1:2, :].astype(F32)
+        c0, c1 = self.ctx[0, r, :], self.ctx[1, r, :]
+        halves = []
+        for n in range(2):
+            w = slice(n * 256, (n + 1) * 256)
+            halves.append(nn(c0, self.w[3, w, :]) + nn(c1, self.w[UNITS + 3, w, :]))
+        o = jnp.concatenate(halves, axis=1)
+        h1 = self.xs[r, :].astype(F32) + o + self.ob[...].astype(F32)
+        self.h1[r, :] = h1
+        n, inv = norm(h1)
+        self.n2[r, :] = n
+        self.r2[r, :] = jnp.broadcast_to(inv, (tile, 128))
+        self.a2[r, :] = (n * gain + shift).astype(BF16)
+
+    def wup(self, m):
+        return (m // 4) * UNITS + 4 + lax.rem(m, 4)
+
+    def wdown(self, m):
+        return (m // 4) * UNITS + 8 + lax.rem(m, 4)
+
+    def up(self, m):
+        u = nn(self.a2[...], self.w[self.wup(m)]) + self.bias_up[m]
+        sg = 0.5 * jnp.tanh(0.851 * u) + 0.5
+        h = u * sg
+        self.hid[m] = h.astype(BF16)
+        self.act[m] = sg + 1.702 * h * (1.0 - sg)
+
+    def down_grad(self, m):
+        w = tn(self.hid[m], self.g[...]).astype(BF16)
+        s, n = m // 4, lax.rem(m, 4)
+        self.grads[n, s, 0:256, :] = w[:, :256]
+        self.grads[n, s, 256:512, :] = w[:, 256:]
+
+    def hidden_back(self, m):
+        w = self.wdown(m)
+        back = nt(self.g[:, 0:256], self.w[w, 0:256, :]) + nt(self.g[:, 256:512], self.w[w, 256:512, :])
+        du = (back * self.act[m]).astype(BF16)
+        self.du[m] = du
+        self.small_up[m] = colsum(du.astype(F32))
+
+    def up_grad(self, m):
+        s, n = m // 4, lax.rem(m, 4)
+        self.grads[4 + n, s] = tn(self.a2[...], self.du[m]).astype(BF16)
+
+    def half_tile(self, i):
+        tile = self.rows // 2
+        r = pl.ds(pl.multiple_of((i // 2) * tile, 16), tile)
+        return r, lax.rem(i, 2)
+
+    def second_grad(self, i):
+        r, n = self.half_tile(i)
+        w = pl.ds(pl.multiple_of(n * 256, 256), 256)
+        acc = None
+        for m in range(8):
+            part = nt(self.du[m, r, :], self.w[(m // 4) * UNITS + 4 + m % 4, w, :])
+            acc = part if acc is None else acc + part
+        self.e[r, w] = acc
+
+    def mlp_out(self, i):
+        r, n = self.half_tile(i)
+        w = pl.ds(pl.multiple_of(n * 256, 256), 256)
+        acc = self.h1[r, w] + self.db[:, w].astype(F32)
+        for m in range(8):
+            acc = acc + nn(self.hid[m, r, :], self.w[(m // 4) * UNITS + 8 + m % 4, w, :])
+        self.h1[r, w] = acc
+
+    def norm_two_back(self):
+        gain = self.gains[1:2, :].astype(F32)
+        zero = jnp.zeros((1, gain.shape[1]), F32)
+        def cap(c, carry):
+            gg, sg, ob, db = carry
+            r = self.crows(c)
+            e, n, g = self.e[r, :], self.n2[r, :], self.g[r, :].astype(F32)
+            dh = g + norm_back(e, n, self.r2[r, 0:1], gain)
+            self.dh1[r, :] = dh
+            dob = dh.astype(BF16)
+            self.dob[r, :] = dob
+            return (gg + colsum(e * n), sg + colsum(e), ob + colsum(dob.astype(F32)), db + colsum(g))
+        gg, sg, ob, db = lax.fori_loop(0, self.caps, cap, (zero, zero, zero, zero))
+        self.small[1:2, :], self.small[3:4, :], self.small[4:5, :], self.small[5:6, :] = gg, sg, ob, db
+
+    def out_back(self, s):
+        w = tn(self.ctx[s], self.dob[...]).astype(BF16)
+        self.grads[8, s, 0:256, :] = w[:, :256]
+        self.grads[8, s, 256:512, :] = w[:, 256:]
+        wo = s * UNITS + 3
+        back = nt(self.dob[:, 0:256], self.w[wo, 0:256, :]) + nt(self.dob[:, 256:512], self.w[wo, 256:512, :])
+        self.dctx[s] = back.astype(BF16)
+
+    def qkv_grad(self, i):
+        s, j = i // 3, lax.rem(i, 3)
+        d = self.dqkv[i]
+        self.grads[9 + j, s] = tn(self.a1[...], d).astype(BF16)
+        self.small_qkv[i] = colsum(d.astype(F32))
+
+    def first_grad(self, i):
+        r, n = self.half_tile(i)
+        w = pl.ds(pl.multiple_of(n * 256, 256), 256)
+        acc = None
+        for m in range(6):
+            part = nt(self.dqkv[m, r, :], self.w[(m // 3) * UNITS + m % 3, w, :])
+            acc = part if acc is None else acc + part
+        self.e[r, w] = acc
+
+    def norm_one_back(self, out, base):
+        gain = self.gains[0:1, :].astype(F32)
+        zero = jnp.zeros((1, gain.shape[1]), F32)
+        gg, sg = zero, zero
+        for c in range(self.caps):
+            r = slice(c * self.pad, (c + 1) * self.pad)
+            e, n = self.e[r, :], self.n1[r, :]
+            dx = self.dh1[r, :] + norm_back(e, n, self.r1[r, 0:1], gain)
+            out[base + c * self.slots : base + (c + 1) * self.slots, :] = dx[: self.slots]
+            gg, sg = gg + colsum(e * n), sg + colsum(e)
+        self.small[0:1, :], self.small[2:3, :] = gg, sg
+
+    def layer_out(self, flat, out):
+        for c in range(self.caps):
+            flat[c * self.slots : (c + 1) * self.slots, :] = self.h1[c * self.pad : c * self.pad + self.slots, :]
+        out[...] = flat[0 : self.caps * self.slots, :].astype(BF16)
+
+    def pack_small(self, out):
+        def put(slot, row, value):
+            for i in range(value.shape[1] // 128):
+                out[slot, row + i : row + i + 1, :] = value[:, i * 128 : (i + 1) * 128]
+        for slot in range(2):
+            out[slot] = jnp.zeros(out.shape[1:], F32)
+            put(slot, 0, self.small_qkv[slot * 3])
+            put(slot, 2, self.small_qkv[slot * 3 + 2])
+            for n in range(4):
+                put(slot, 4 + 2 * n, self.small_up[slot * 4 + n])
+            for i, k in enumerate((4, 5, 0, 1, 2, 3)):
+                put(slot, 12 + 4 * i, self.small[k : k + 1, :])
+
+
+class Peers:
+    def __init__(self):
+        dp, t = lax.axis_index("dp"), lax.axis_index("tensor")
+        depth = lax.axis_size("dp") // 4
+        self.core = lax.rem(dp, 2)
+        self.x = lax.rem(dp // 2, 2)
+        self.z = dp // 4
+        self.t = t
+        self.to_y = (dp, 1 - t)
+        self.to_x = (dp + 2 - 4 * self.x, t)
+        self.to_core = (dp + 1 - 2 * self.core, t)
+        self.depth = depth
+        self.to_z = [(lax.rem(self.z + k, depth) * 4 + lax.rem(dp, 4), t) for k in range(1, depth)]
+        self.z_of = [lax.rem(self.z + k, depth) for k in range(1, depth)]
+
+    def all(self):
+        return [self.to_y, self.to_x, self.to_core] + self.to_z
+
+    def meet(self):
+        barrier = pltpu.get_barrier_semaphore()
+        peers = self.all()
+        for peer in peers:
+            pl.semaphore_signal(barrier, inc=1, device_id=peer, device_id_type=MESH)
+        pl.semaphore_wait(barrier, len(peers))
+
+
+def rows(index, size):
+    return pl.ds(pl.multiple_of(index * size, size), size)
+
+
+def remote(src, dst, send, recv, peer):
+    return pltpu.make_async_remote_copy(src_ref=src, dst_ref=dst, send_sem=send, recv_sem=recv, device_id=peer, device_id_type=MESH)
+
+
+class Weights:
+    def __init__(self, peers, w, send, recv):
+        self.p, self.w, self.send, self.recv = peers, w, send, recv
+        self.quarter = peers.core * 2 + peers.x
+        self.size = w.shape[1] // 4
+
+    def y(self, u):
+        r = rows(self.quarter, self.size)
+        return remote(self.w.at[u, r], self.w.at[UNITS + u, r], self.send.at[u, 0], self.recv.at[u, 0], self.p.to_y)
+
+    def x(self, u):
+        part = self.w.at[UNITS + u, rows(self.quarter, self.size)]
+        return remote(part, part, self.send.at[u, 1], self.recv.at[u, 1], self.p.to_x)
+
+    def c(self, u):
+        part = self.w.at[UNITS + u, rows(self.p.core, self.size * 2)]
+        return remote(part, part, self.send.at[u, 2], self.recv.at[u, 2], self.p.to_core)
+
+    def relay_x(self, u):
+        self.y(u).wait_recv()
+        self.x(u).start()
+
+    def relay_c(self, u):
+        self.x(u).wait_recv()
+        self.c(u).start()
+
+    def ready(self, u):
+        self.c(u).wait_recv()
+
+    def drain(self, u):
+        self.y(u).wait_send()
+        self.x(u).wait_send()
+        self.c(u).wait_send()
+
+
+class Reduce:
+    def __init__(self, peers, refs, sem0, send, recv):
+        self.p = peers
+        self.g, self.cr, self.yr, self.xr, self.zr, self.f = refs
+        self.sem0, self.send, self.recv = sem0, send, recv
+        self.count = self.g.shape[0]
+        self.full = self.g.shape[2]
+        self.half, self.quarter = self.full // 2, self.full // 4
+        self.shard = self.quarter // peers.depth
+
+    def sems(self, n, k):
+        return self.send.at[self.sem0 + n, k], self.recv.at[self.sem0 + n, k]
+
+    def c(self, n):
+        return remote(self.g.at[n, :, rows(1 - self.p.core, self.half)], self.cr.at[n], *self.sems(n, 0), self.p.to_core)
+
+    def y(self, n):
+        return remote(self.cr.at[n, 1], self.yr.at[n], *self.sems(n, 1), self.p.to_y)
+
+    def x(self, n):
+        return remote(self.cr.at[n, 0, rows(1 - self.p.x, self.quarter)], self.xr.at[n], *self.sems(n, 2), self.p.to_x)
+
+    def z(self, n):
+        return [
+            remote(
+                self.cr.at[n, 0, pl.ds(pl.multiple_of(self.p.x * self.quarter + self.p.z_of[k] * self.shard, self.shard), self.shard)],
+                self.zr.at[n, k],
+                *self.sems(n, 5 + k),
+                self.p.to_z[k],
+            )
+            for k in range(self.p.depth - 1)
+        ]
+
+    def own_shard(self):
+        p = self.p
+        return pl.ds(pl.multiple_of(p.core * self.half + p.x * self.quarter + p.z * self.shard, self.shard), self.shard)
+
+    def za(self, n):
+        part = self.f.at[n, self.own_shard()]
+        return [
+            remote(part, part, *self.sems(n, 4 + self.p.depth + k), self.p.to_z[k]) for k in range(self.p.depth - 1)
+        ]
+
+    def xa(self, n):
+        part = self.f.at[n, pl.ds(pl.multiple_of(self.p.core * self.half + self.p.x * self.quarter, self.quarter), self.quarter)]
+        return remote(part, part, *self.sems(n, 3), self.p.to_x)
+
+    def ca(self, n):
+        part = self.f.at[n, rows(self.p.core, self.half)]
+        return remote(part, part, *self.sems(n, 4), self.p.to_core)
+
+    def c_start(self, n):
+        self.c(n).start()
+
+    def c_done(self, n):
+        self.c(n).wait_recv()
+        self.cr[n] = self.cr[n] + self.g[n, :, rows(self.p.core, self.half), :]
+        self.y(n).start()
+
+    def y_done(self, n):
+        self.y(n).wait_recv()
+        self.cr[n, 0] = self.cr[n, 0] + self.yr[n]
+        self.x(n).start()
+
+    def x_done(self, n):
+        self.x(n).wait_recv()
+        r = rows(self.p.x, self.quarter)
+        self.cr[n, 0, r, :] = self.cr[n, 0, r, :] + self.xr[n]
+        for copy in self.z(n):
+            copy.start()
+
+    def z_done(self, n):
+        for copy in self.z(n):
+            copy.wait_recv()
+        mine = pl.ds(pl.multiple_of(self.p.x * self.quarter + self.p.z * self.shard, self.shard), self.shard)
+        total = self.cr[n, 0, mine, :].astype(F32)
+        for k in range(self.p.depth - 1):
+            total = total + self.zr[n, k].astype(F32)
+        self.f[n, self.own_shard(), :] = total.astype(self.f.dtype)
+        for copy in self.za(n):
+            copy.start()
+
+    def za_done(self, n):
+        for copy in self.za(n):
+            copy.wait_recv()
+        self.xa(n).start()
+
+    def xa_done(self, n):
+        self.xa(n).wait_recv()
+        self.ca(n).start()
+
+    def ca_done(self, n):
+        self.ca(n).wait_recv()
+
+    def drain(self, n):
+        for copy in [self.c(n), self.y(n), self.x(n), self.xa(n), self.ca(n)] + self.z(n) + self.za(n):
+            copy.wait_send()
+
+
+STAGES = ("y_done", "x_done", "z_done", "za_done", "xa_done", "ca_done")
+
+
+def step(big, small, outs, tick):
+    for lag, name in enumerate(STAGES):
+        unit = tick - lag
+
+        @pl.when((unit >= 0) & (unit < UNITS))
+        def _():
+            getattr(big, name)(unit)
+            if name == "ca_done":
+                outs(unit).start()
+
+        if small is not None:
+
+            @pl.when(unit == UNITS)
+            def _():
+                getattr(small, name)(0)
+
+
+def kernel(caps, slots, pad, names_in, *all_refs):
+    L = Layer(caps, slots, pad, dict(zip(names_in, all_refs)))
+    peers = Peers()
+    L.cap_base = peers.t * caps
+    weights = Weights(peers, L.w, L.wsend, L.wrecv)
+    big = Reduce(peers, (L.grads, L.cr, L.yr, L.xr, L.zr, L.f), 0, L.gsend, L.grecv)
+    small = Reduce(peers, (L.sg, L.scr, L.syr, L.sxr, L.szr, L.sf), UNITS, L.gsend, L.grecv)
+
+    local = []
+
+    def load(a, b):
+        copy = pltpu.make_async_copy(a, b, L.lsem.at[len(local)])
+        copy.start()
+        local.append(copy)
+
+    for j in range(3):
+        load(L.wqkv_a.at[j], L.w.at[j])
+    for n in range(2):
+        load(L.wo_a.at[:, pl.ds(n * 256, 256)], L.w.at[3, pl.ds(n * 256, 256)])
+    load(L.tok, L.tok_v)
+    for n in range(4):
+        load(L.wu_a.at[:, pl.ds(n * 256, 256)], L.w.at[4 + n])
+    for n in range(4):
+        for k in range(2):
+            load(L.wd_a.at[pl.ds(n * 256, 256), pl.ds(k * 256, 256)], L.w.at[8 + n, pl.ds(k * 256, 256)])
+    load(L.cot, L.cot_v)
+    peers.meet()
+    bias_send = [
+        remote(L.qvb, L.qvb_b, L.bsem.at[0], L.bsem.at[1], peers.to_y),
+        remote(L.ub, L.ub_b, L.bsem.at[2], L.bsem.at[3], peers.to_y),
+    ]
+    for copy in bias_send:
+        copy.start()
+    for copy in local:
+        copy.wait()
+    loop(UNITS, lambda u: weights.y(u).start())
+    L.widen(L.tok_v, peers.t * caps * slots, L.xs)
+    L.norm_one()
+    for copy in bias_send:
+        copy.wait()
+    for s, (qvb, ub) in enumerate(((L.qvb, L.ub), (L.qvb_b, L.ub_b))):
+        for j in range(3):
+            if j == 1:
+                L.bias_qkv[s * 3 + j] = jnp.zeros((1, 256), F32)
+            else:
+                L.bias_qkv[s * 3 + j] = qvb[j // 2 : j // 2 + 1, :].astype(F32)
+        for n in range(4):
+            L.bias_up[s * 4 + n] = ub[:, n * 256 : (n + 1) * 256].astype(F32)
+    loop(3, L.qkv)
+    loop(2, weights.relay_x)
+
+    def attend_own(i):
+        L.attention(i)
+
+        @pl.when(i < 7)
+        def _():
+            weights.relay_x(2 + i)
+
+        @pl.when(i < 8)
+        def _():
+            weights.relay_c(i)
+
+    loop(caps, attend_own)
+    L.widen(L.cot_v, peers.t * caps * slots, L.g)
+    loop(3, lambda i: (weights.ready(i), L.qkv(3 + i)))
+
+    def attend_other(i):
+        L.attention(caps + i)
+
+        @pl.when(i < 3)
+        def _():
+            weights.relay_x(9 + i)
+
+        @pl.when(i < 4)
+        def _():
+            weights.relay_c(8 + i)
+
+    loop(caps, attend_other)
+    weights.ready(3)
+    loop(4, L.project)
+    loop(4, L.up)
+    loop(4, lambda i: (weights.ready(4 + i), L.up(4 + i)))
+
+    def down(i):
+        L.down_grad(i)
+        L.down_grad(4 + i)
+        big.c_start(i)
+
+        @pl.when(i > 0)
+        def _():
+            big.c_done(i - 1)
+
+    loop(4, down)
+    loop(4, L.hidden_back)
+    big.c_done(3)
+    loop(4, lambda i: (weights.ready(8 + i), L.hidden_back(4 + i)))
+
+    outs = lambda n: pltpu.make_async_copy(L.f.at[n], L.f_out.at[n], L.osem.at[n])
+    tick = functools.partial(step, big, None, outs)
+
+    def ups(i):
+        L.up_grad(i)
+        L.up_grad(4 + i)
+        big.c_start(4 + i)
+
+        @pl.when(i > 0)
+        def _():
+            big.c_done(3 + i)
+
+        @pl.when(lax.rem(i, 2) == 1)
+        def _():
+            tick(i // 2)
+
+    loop(4, ups)
+    loop(4, L.second_grad)
+    big.c_done(7)
+    tick(2)
+    L.norm_two_back()
+    loop(2, L.out_back)
+    big.c_start(8)
+    tick(3)
+
+    def attend_back(i):
+        L.attention_back(i)
+
+        @pl.when(i == 1)
+        def _():
+            big.c_done(8)
+
+        @pl.when(lax.rem(i, 6) == 5)
+        def _():
+            tick(4 + i // 6)
+
+    loop(2 * caps, attend_back)
+
+    def qkvs(i):
+        L.qkv_grad(i)
+        L.qkv_grad(3 + i)
+        big.c_start(9 + i)
+
+        @pl.when(i > 0)
+        def _():
+            big.c_done(8 + i)
+
+    loop(3, qkvs)
+    tick(6)
+    loop(4, L.first_grad)
+    big.c_done(11)
+    size = caps * slots
+    base = (size + 7) // 8 * 8
+    L.norm_one_back(L.stage, base)
+    dx_copy = pltpu.make_async_copy(L.stage.at[pl.ds(base, size)], L.dx_out, L.osem.at[UNITS])
+    dx_copy.start()
+    L.pack_small(L.sg.at[0])
+    small.c_start(0)
+    tick(7)
+    loop(4, L.mlp_out)
+    L.layer_out(L.stage, L.yb)
+    y_copy = pltpu.make_async_copy(L.yb, L.y_out, L.osem.at[UNITS + 1])
+    y_copy.start()
+    small.c_done(0)
+    loop(UNITS + len(STAGES) - 8, lambda i: step(big, small, outs, 8 + i))
+    s_copy = pltpu.make_async_copy(L.sf.at[0], L.s_out, L.osem.at[UNITS + 2])
+    s_copy.start()
+
+    def drain(n):
+        weights.drain(n)
+        big.drain(n)
+        outs(n).wait()
+
+    loop(UNITS, drain)
+    small.drain(0)
+    dx_copy.wait()
+    y_copy.wait()
+    s_copy.wait()
+
+
+def finish(f, s, y, dx, y_out, dx_out, qkv, out, up, down, qvb, ob, ub, db, gg, sh, f_v, wide, sem_in, sem_out, sem_io):
+    ins = [pltpu.make_async_copy(f.at[n], f_v.at[n], sem_in.at[n]) for n in range(UNITS)]
+    for copy in ins:
+        copy.start()
+    io = [pltpu.make_async_copy(y, y_out, sem_io.at[0]), pltpu.make_async_copy(dx, dx_out, sem_io.at[1])]
+    for copy in io:
+        copy.start()
+    for n in range(UNITS):
+        ins[n].wait()
+        wide[n] = f_v[n].astype(F32)
+        if n < 4 or n == 8:
+            parts = []
+            for k in range(2):
+                c = pl.ds(k * 256, 256)
+                dst = down.at[pl.ds(n * 256, 256), c] if n < 4 else out.at[:, c]
+                parts.append((wide.at[n, c], dst))
+        elif n < 8:
+            parts = [(wide.at[n], up.at[:, pl.ds((n - 4) * 256, 256)])]
+        else:
+            parts = [(wide.at[n], qkv.at[n - 9])]
+        for k, (a, b) in enumerate(parts):
+            copy = pltpu.make_async_copy(a, b, sem_out.at[2 * n + k])
+            copy.start()
+            io.append(copy)
+
+    def row(first, count):
+        return jnp.concatenate([s[first + i : first + i + 1, :] for i in range(count)], axis=1)
+
+    qvb[0:1, :], qvb[1:2, :] = row(0, 2), row(2, 2)
+    ub[...] = row(4, 8)
+    ob[...], db[...] = row(12, 4), row(16, 4)
+    gg[0:1, :], gg[1:2, :] = row(20, 4), row(24, 4)
+    sh[0:1, :], sh[1:2, :] = row(28, 4), row(32, 4)
+    for copy in io:
+        copy.wait()
+
+
+def shards(depth, tokens, lengths, qkv_weight, qv_bias, out_weight, out_bias, up_weight, up_bias, down_weight, down_bias, norm_gain, norm_shift, cotangent):
+    total, width = tokens.shape
+    count = lengths.shape[0]
+    slots = total // count
+    caps = count // 2
+    pad = (slots + 15) // 16 * 16
+    rws = caps * pad
+    V = pl.BlockSpec(memory_space=pltpu.VMEM)
+    A = pl.BlockSpec(memory_space=pl.ANY)
+    S = pl.BlockSpec(memory_space=pltpu.SMEM)
+    ins = [
+        ("tok", tokens, A), ("cot", cotangent, A), ("lengths", lengths, S),
+        ("wqkv_a", qkv_weight, A), ("wo_a", out_weight, A), ("wu_a", up_weight, A), ("wd_a", down_weight, A),
+        ("qvb", qv_bias, V), ("ub", up_bias[None], V),
+        ("ob", out_bias[None], V), ("db", down_bias[None], V), ("gains", norm_gain, V), ("shifts", norm_shift, V),
+    ]
+    outs = [
+        ("y_out", (caps * slots, 512), BF16), ("dx_out", (caps * slots, 512), F32),
+        ("f_out", (UNITS, 512, 256), BF16), ("s_out", (128, 128), F32),
+    ]
+    vm = pltpu.VMEM
+    sems = UNITS + 1, 3 + 2 * depth
+    scr = [
+        ("tok_v", vm((total, 512), BF16)), ("cot_v", vm((total, 512), BF16)),
+        ("stage", vm((total + 16, 512), F32)), ("xs", vm((rws, 512), BF16)), ("g", vm((rws, 512), BF16)),
+        ("n1", vm((rws, 512), F32)), ("r1", vm((rws, 128), F32)), ("a1", vm((rws, 512), BF16)),
+        ("w", vm((2 * UNITS, 512, 256), BF16)), ("qvb_b", vm((2, 256), BF16)), ("ub_b", vm((1, 1024), BF16)),
+        ("bias_qkv", vm((6, 1, 256), F32)), ("bias_up", vm((8, 1, 256), F32)),
+        ("pqkv", vm((6, rws, 256), BF16)), ("probs", vm((2 * caps, 4 * pad, pad), F32)), ("ctx", vm((2, rws, 256), BF16)),
+        ("h1", vm((rws, 512), F32)), ("n2", vm((rws, 512), F32)), ("r2", vm((rws, 128), F32)), ("a2", vm((rws, 512), BF16)),
+        ("hid", vm((8, rws, 256), BF16)), ("act", vm((8, rws, 256), F32)), ("du", vm((8, rws, 256), BF16)),
+        ("e", vm((rws, 512), F32)), ("dh1", vm((rws, 512), F32)), ("dob", vm((rws, 512), BF16)), ("dctx", vm((2, rws, 256), BF16)),
+        ("dqkv", vm((6, rws, 256), BF16)), ("yb", vm((caps * slots, 512), BF16)),
+        ("small", vm((8, 512), F32)), ("small_up", vm((8, 1, 256), F32)), ("small_qkv", vm((6, 1, 256), F32)),
+        ("grads", vm((UNITS, 2, 512, 256), BF16)), ("cr", vm((UNITS, 2, 256, 256), BF16)), ("yr", vm((UNITS, 256, 256), BF16)),
+        ("xr", vm((UNITS, 128, 256), BF16)), ("zr", vm((UNITS, depth - 1, 128 // depth, 256), BF16)), ("f", vm((UNITS, 512, 256), BF16)),
+        ("sg", vm((1, 2, 128, 128), F32)), ("scr", vm((1, 2, 64, 128), F32)), ("syr", vm((1, 64, 128), F32)),
+        ("sxr", vm((1, 32, 128), F32)), ("szr", vm((1, depth - 1, 32 // depth, 128), F32)), ("sf", vm((1, 128, 128), F32)),
+        ("lsem", pltpu.SemaphoreType.DMA((20,))), ("osem", pltpu.SemaphoreType.DMA((UNITS + 3,))), ("bsem", pltpu.SemaphoreType.DMA((4,))),
+        ("wsend", pltpu.SemaphoreType.DMA((UNITS, 3))), ("wrecv", pltpu.SemaphoreType.DMA((UNITS, 3))),
+        ("gsend", pltpu.SemaphoreType.DMA(sems)), ("grecv", pltpu.SemaphoreType.DMA(sems)),
+    ]
+    names = [n for n, _, _ in ins] + [n for n, _, _ in outs] + [n for n, _ in scr]
+    y, dx, f, s = pl.pallas_call(
+        functools.partial(kernel, caps, slots, pad, names),
+        out_shape=[jax.ShapeDtypeStruct(s, d) for _, s, d in outs],
+        in_specs=[s for _, _, s in ins],
+        out_specs=[A] * len(outs),
+        scratch_shapes=[s for _, s in scr],
+        compiler_params=pltpu.CompilerParams(vmem_limit_bytes=61 << 20, collective_id=0, has_side_effects=True),
+        name="layer",
+    )(*[v for _, v, _ in ins])
+    results = [
+        (y.shape, BF16, A), (dx.shape, F32, A), (qkv_weight.shape, F32, A), (out_weight.shape, F32, A),
+        (up_weight.shape, F32, A), (down_weight.shape, F32, A),
+        (qv_bias.shape, F32, V), ((1, 512), F32, V), ((1, up_bias.shape[0]), F32, V), ((1, 512), F32, V), ((2, 512), F32, V), ((2, 512), F32, V),
+    ]
+    y, dx, qkv, out, up, down, qvb, ob, ub, db, gg, sh = pl.pallas_call(
+        finish,
+        out_shape=[jax.ShapeDtypeStruct(s, d) for s, d, _ in results],
+        in_specs=[A, V, A, A],
+        out_specs=[s for _, _, s in results],
+        scratch_shapes=[
+            vm((UNITS, 512, 256), BF16), vm((UNITS, 512, 256), F32),
+            pltpu.SemaphoreType.DMA((UNITS,)), pltpu.SemaphoreType.DMA((2 * UNITS,)), pltpu.SemaphoreType.DMA((2,)),
+        ],
+        compiler_params=pltpu.CompilerParams(vmem_limit_bytes=24 << 20),
+        name="finish",
+    )(f, s, y, dx)
+    return y, dx, qkv, qvb, out, ob[0], up, ub[0], down, db[0], gg, sh
 
 
 def matmul_plain(left, right):
@@ -25,13 +774,13 @@
     )
 
 
-def norm_stats(values):
+def plain_norm_stats(values):
     center = values - jnp.mean(values, axis=-1, keepdims=True)
     inv_std = lax.rsqrt(jnp.mean(center * center, axis=-1, keepdims=True) + EPSILON)
     return (center * inv_std, inv_std)
 
 
-def norm_back(upstream, normed, inv_std, gain_vec):
+def plain_norm_back(upstream, normed, inv_std, gain_vec):
     scaled = upstream * gain_vec
     inner_mean = jnp.mean(scaled * normed, axis=-1, keepdims=True)
     result = inv_std * (scaled - jnp.mean(scaled, axis=-1, keepdims=True) - normed * inner_mean)
@@ -42,7 +791,7 @@
     return lax.dynamic_slice_in_dim(values, row_start, share_rows, 0)
 
 
-def shards(
+def shards_by_heads(
     tokens,
     lengths,
     qkv_weight,
@@ -71,7 +820,7 @@
     score_scale = HD ** (-0.5)
     qv_float = qv_bias.astype(jnp.float32)
     token_f = tokens.astype(jnp.float32)
-    normed_one, inv_one = norm_stats(token_f)
+    normed_one, inv_one = plain_norm_stats(token_f)
     first_in = (normed_one * gains[0] + shifts[0]).astype(jnp.bfloat16)
     queries = (matmul_plain(first_in, qkv_weight[0]) + qv_float[0]).astype(jnp.bfloat16)
     keys_all = matmul_plain(first_in, qkv_weight[1]).astype(jnp.bfloat16)
@@ -103,7 +852,7 @@
     attn_part = matmul_plain(context, out_weight)
     attn_out = lax.psum(attn_part, "tensor") + out_bias.astype(jnp.float32)
     hidden_res = token_f + attn_out
-    normed_two, inv_two = norm_stats(hidden_res)
+    normed_two, inv_two = plain_norm_stats(hidden_res)
     second_in = (normed_two * gains[1] + shifts[1]).astype(jnp.bfloat16)
     upper = matmul_plain(second_in, up_weight) + up_bias.astype(jnp.float32)
     sigma = jax.nn.sigmoid(1.702 * upper)
@@ -126,7 +875,7 @@
     up_bias_grad = jnp.sum(upper_grad.astype(jnp.float32), axis=0)
     second_part = contract_cols(upper_grad, up_weight)
     second_grad = lax.psum(second_part, "tensor")
-    residual_back, gain_two, shift_two = norm_back(second_grad, normed_two, inv_two, gains[1])
+    residual_back, gain_two, shift_two = plain_norm_back(second_grad, normed_two, inv_two, gains[1])
     residual_full = grad_f + residual_back
     branch_grad = residual_full.astype(jnp.bfloat16)
     out_bias_grad = jnp.sum(branch_grad.astype(jnp.float32), axis=0)
@@ -172,7 +921,7 @@
         + contract_cols(value_grad, qkv_weight[2])
     )
     first_grad = lax.psum(first_part.astype(jnp.bfloat16), "tensor").astype(jnp.float32)
-    input_back, gain_one, shift_one = norm_back(first_grad, normed_one, inv_one, gains[0])
+    input_back, gain_one, shift_one = plain_norm_back(first_grad, normed_one, inv_one, gains[0])
     input_grad = row_slice(residual_full + input_back, row_start, share_rows)
     gain_grads = jnp.stack([gain_one, gain_two])
     shift_grads = jnp.stack([shift_one, shift_two])
@@ -205,37 +954,15 @@
 
 
 def solution(mesh):
+    dp, tensor = mesh.shape["dp"], mesh.shape["tensor"]
+    if tensor == 2 and dp == 16:
+        body = functools.partial(shards, dp // 4)
+    else:
+        body = shards_by_heads
     return jax.shard_map(
-        shards,
+        body,
         mesh=mesh,
-        in_specs=(
-            P("dp", None),
-            P("dp"),
-            P(None, None, "tensor"),
-            P(None, "tensor"),
-            P("tensor", None),
-            P(),
-            P(None, "tensor"),
-            P("tensor"),
-            P("tensor", None),
-            P(),
-            P(),
-            P(),
-            P("dp", None),
-        ),
-        out_specs=(
-            P(("dp", "tensor"), None),
-            P(("dp", "tensor"), None),
-            P(None, None, "tensor"),
-            P(None, "tensor"),
-            P("tensor", None),
-            P(),
-            P(None, "tensor"),
-            P("tensor"),
-            P("tensor", None),
-            P(),
-            P(),
-            P(),
-        ),
+        in_specs=(P("dp", None), P("dp"), P(None, None, "tensor"), P(None, "tensor"), P("tensor", None), P(), P(None, "tensor"), P("tensor"), P("tensor", None), P(), P(), P(), P("dp", None)),
+        out_specs=(P(("dp", "tensor"), None), P(("dp", "tensor"), None), P(None, None, "tensor"), P(None, "tensor"), P("tensor", None), P(), P(None, "tensor"), P("tensor"), P("tensor", None), P(), P(), P()),
         check_vma=False,
     )

time: 488 us -> 124 us (0.25); the launches traced: 479 us -> 123 us
  waiting for transfers between devices: 302 us -> 0 us
  Pallas kernels: 0 us -> 114 us
  matrix products: 49.8 us -> 0 us
  other arithmetic: 37.6 us -> 0 us
  blocking collectives: 34.1 us -> 0 us
  local copies, waits for them, and re-layouts: 39.9 us -> 8.89 us
  between operations: 14.9 us -> 0.66 us
    psum x4 -> x0, waiting for transfers between devices: 302 us -> none  [the longest x1 96.2 us: shards(): lax.psum(qkv_grad.astype(jnp.bfloat16), 'dp').astype(jnp.float32)]
    pallas_call x0 -> x2, Pallas kernels: none -> 114 us  [the longest x1 109 us: shards(): pl.pallas_call(functools.partial(kernel, caps, slots, pad, names), out_sh...]
    dot_general x24 -> x0, matrix products: 49.8 us -> none  [the longest x6 16.2 us: contract_rows(): lax.dot_general(left, right, (((0,), (0,)), ((), ())), preferred_element_...]
    psum x1 -> x0, blocking collectives: 34.1 us -> none  [shards(): lax.psum(qv_bias_grad.astype(jnp.bfloat16), 'dp').astype(jnp.float32)]
    reshape x8 -> x0, local copies, waits for them, and re-layouts: 22.3 us -> none  [the longest x2 6.65 us: shards(): key_four = keys_all.reshape(shape4)]
    reduce_sum x9 -> x0, other arithmetic: 17.8 us -> none  [the longest x2 8.64 us: norm_back(): jnp.sum(upstream * normed, axis=0)]
    convert_element_type x15 -> x0, other arithmetic: 12.4 us -> none  [the longest x1 2.5 us: shards(): lax.psum(qkv_grad.astype(jnp.bfloat16), 'dp').astype(jnp.float32)]
    convert_element_type x8 -> x0, local copies, waits for them, and re-layouts: 9.88 us -> none  [the longest x2 3.86 us: shards(): context = context.reshape(total_rows, local_width).astype(jnp.bfloat16)]
  transfers between devices with their start and end apart: 4 -> 0, of which waited for: 4 -> 0; matrix products, arithmetic and copies ran while one was open for 5% -> 0% of each run, Pallas kernels for 0% -> 0%
where the time goes in v1:
time: 124 us; the launch traced here: 123 us
  Pallas kernels  114 us (92%)
  local copies, waits for them, and re-layouts  8.89 us (7%)
    pallas_call x1, Pallas kernels, shards(): pl.pallas_call(functools.partial(kernel, caps, slots, pad, names), out_sh...  109 us
    unnamed x8, local copies, waits for them, and re-layouts  5.1 us
    pallas_call x1, Pallas kernels, shards(): pl.pallas_call(finish, out_shape=[jax.ShapeDtypeStruct(s, d) for s, d, _...  4.38 us

profile of v1, /device:TPU:0, one launch (start us, length us, event | category | flops | bytes accessed | tf_op | source)
XLA Modules:
  0.0 123.2 jit_solution(17788226878240588111)
XLA Ops:
  0.6 1.3 %broadcast_in_dim.10.all_refs_9_ = bf16[1,512]{1,0:T(2,128)(2,1)} reshape(bf16[512]{0:T(512)(128)(2,1)} %param.18) | data formatting | bytes 2048 | tf_op jit(solution)/shard_map/broadcast_in_dim | solution.py:703
  1.9 1.3 %broadcast_in_dim.11.all_refs_10_ = bf16[1,512]{1,0:T(2,128)(2,1)} reshape(bf16[512]{0:T(512)(128)(2,1)} %param.22) | data formatting | bytes 2048 | tf_op jit(solution)/shard_map/broadcast_in_dim | solution.py:703
  3.2 1.3 %broadcast_in_dim.9.all_refs_8_ = bf16[1,1024]{1,0:T(2,128)(2,1)} reshape(bf16[1024]{0:T(1024)(128)(2,1)} %param.20) | data formatting | bytes 4096 | tf_op jit(solution)/shard_map/broadcast_in_dim | solution.py:702
  4.4 109.2 %layer.1 = (bf16[616,512]{1,0:T(8,128)(2,1)}, f32[616,512]{1,0:T(8,128)}, bf16[12,512,256]{2,1,0:T(8,128)(2,1)}, f32[128,128]{1,0:T(8,128)}) custom-call(bf16[1232,512]{1,0:T(8,128)(2,1)} %all_refs_0_.1, bf16[1232,512]{1,0:T(8,128)(2,1)} %all_refs_1_.1, s32[16]{0:T(128)} %all_refs_2_.1, bf16[3,512,256]{2,1,0:T(8,128)(2,1)} %all_refs_3_.1, ...), custom_call_target="tpu_custom_call" | custom-call | tf_op jit(solution)/shard_map/layer/pallas_call | solution.py:732
  113.7 0.0 copy-start
  113.7 1.9 %copy-done = bf16[12,512,256]{2,1,0:T(8,128)(2,1)S(1)} copy-done((bf16[12,512,256]{2,1,0:T(8,128)(2,1)S(1)}, bf16[12,512,256]{2,1,0:T(8,128)(2,1)}, u32[]{:S(2)}) %copy-start) | copy-done | bytes 3145752
  115.6 0.0 copy-start.1
  115.6 1.3 %copy-done.1 = f32[616,512]{1,0:T(8,128)S(1)} copy-done((f32[616,512]{1,0:T(8,128)S(1)}, f32[616,512]{1,0:T(8,128)}, u32[]{:S(2)}) %copy-start.1) | copy-done | bytes 1261592
  116.9 0.0 copy-start.2
  116.9 1.1 copy-done.2
  118.0 0.0 copy-start.3
  118.0 0.8 copy-done.3
  118.8 4.4 %finish.1 = (bf16[616,512]{1,0:T(8,128)(2,1)}, f32[616,512]{1,0:T(8,128)}, f32[3,512,256]{2,1,0:T(8,128)}, f32[256,512]{1,0:T(8,128)}, f32[512,1024]{1,0:T(8,128...) custom-call(bf16[12,512,256]{2,1,0:T(8,128)(2,1)S(1)} %copy-done, ...), custom_call_target="tpu_custom_call" | custom-call | tf_op jit(solution)/shard_map/finish/pallas_call | solution.py:746
Async XLA Ops:
  113.7 1.9 %copy-start = (bf16[12,512,256]{2,1,0:T(8,128)(2,1)S(1)}, bf16[12,512,256]{2,1,0:T(8,128)(2,1)}, u32[]{:S(2)}) copy-start(bf16[12,512,256]{2,1,0:T(8,128)(2,1)} %get-tuple-element.28.f) | copy-start | bytes 9437188
  115.6 1.3 %copy-start.1 = (f32[616,512]{1,0:T(8,128)S(1)}, f32[616,512]{1,0:T(8,128)}, u32[]{:S(2)}) copy-start(f32[616,512]{1,0:T(8,128)} %get-tuple-element.31.dx) | copy-start | bytes 3784708
  116.9 1.1 copy-start.2
  118.0 0.8 copy-start.3

commit v2 on v1

--- a/solution.py
+++ b/solution.py
@@ -13,6 +13,8 @@
 BF16 = jnp.bfloat16
 LOG2E = 1.4426950408889634
 UNITS = 12
+EARLY = 9
+LAG = 2
 MESH = pl.DeviceIdType.MESH
 
 
@@ -101,6 +103,16 @@
             self.r1[r, :] = jnp.broadcast_to(inv, (self.pad, 128))
             self.a1[r, :] = (n * gain + shift).astype(BF16)
         loop(self.caps, cap)
+
+    def biases(self, s, qvb, ub):
+        for j in range(3):
+            if j == 1:
+                self.bias_qkv[s * 3 + j] = jnp.zeros((1, 256), F32)
+            else:
+                self.bias_qkv[s * 3 + j] = qvb[j // 2 : j // 2 + 1, :].astype(F32)
+        up = ub[...].astype(F32).reshape(1, -1)
+        for n in range(4):
+            self.bias_up[s * 4 + n] = up[:, n * 256 : (n + 1) * 256]
 
     def qkv(self, i):
         s, j = i // 3, lax.rem(i, 3)
@@ -156,7 +168,7 @@
             w = slice(n * 256, (n + 1) * 256)
             halves.append(nn(c0, self.w[3, w, :]) + nn(c1, self.w[UNITS + 3, w, :]))
         o = jnp.concatenate(halves, axis=1)
-        h1 = self.xs[r, :].astype(F32) + o + self.ob[...].astype(F32)
+        h1 = self.xs[r, :].astype(F32) + o + self.ob[...].astype(F32).reshape(1, -1)
         self.h1[r, :] = h1
         n, inv = norm(h1)
         self.n2[r, :] = n
@@ -210,7 +222,7 @@
     def mlp_out(self, i):
         r, n = self.half_tile(i)
         w = pl.ds(pl.multiple_of(n * 256, 256), 256)
-        acc = self.h1[r, w] + self.db[:, w].astype(F32)
+        acc = self.h1[r, w] + self.db[w].astype(F32).reshape(1, -1)
         for m in range(8):
             acc = acc + nn(self.hid[m, r, :], self.w[(m // 4) * UNITS + 8 + m % 4, w, :])
         self.h1[r, w] = acc
@@ -302,12 +314,13 @@
     def all(self):
         return [self.to_y, self.to_x, self.to_core] + self.to_z
 
+    def greet(self):
+        barrier = pltpu.get_barrier_semaphore()
+        for peer in self.all():
+            pl.semaphore_signal(barrier, inc=1, device_id=peer, device_id_type=MESH)
+
     def meet(self):
-        barrier = pltpu.get_barrier_semaphore()
-        peers = self.all()
-        for peer in peers:
-            pl.semaphore_signal(barrier, inc=1, device_id=peer, device_id_type=MESH)
-        pl.semaphore_wait(barrier, len(peers))
+        pl.semaphore_wait(pltpu.get_barrier_semaphore(), len(self.all()))
 
 
 def rows(index, size):
@@ -344,6 +357,12 @@
         self.x(u).wait_recv()
         self.c(u).start()
 
+    def tick(self, u):
+        if u < UNITS:
+            self.relay_x(u)
+        if 2 <= u < UNITS + 2:
+            self.relay_c(u - 2)
+
     def ready(self, u):
         self.c(u).wait_recv()
 
@@ -354,9 +373,10 @@
 
 
 class Reduce:
-    def __init__(self, peers, refs, sem0, send, recv):
+    def __init__(self, peers, refs, sem0, send, recv, across=None):
         self.p = peers
         self.g, self.cr, self.yr, self.xr, self.zr, self.f = refs
+        self.x2r, self.y2r = across or (None, None)
         self.sem0, self.send, self.recv = sem0, send, recv
         self.count = self.g.shape[0]
         self.full = self.g.shape[2]
@@ -374,6 +394,14 @@
 
     def x(self, n):
         return remote(self.cr.at[n, 0, rows(1 - self.p.x, self.quarter)], self.xr.at[n], *self.sems(n, 2), self.p.to_x)
+
+    def x2(self, n):
+        return remote(
+            self.cr.at[n, :, rows(1 - self.p.x, self.quarter)], self.x2r.at[n - EARLY], *self.sems(n, 2), self.p.to_x
+        )
+
+    def y2(self, n):
+        return remote(self.cr.at[n, 1, rows(self.p.x, self.quarter)], self.y2r.at[n - EARLY], *self.sems(n, 1), self.p.to_y)
 
     def z(self, n):
         return [
@@ -407,10 +435,30 @@
     def c_start(self, n):
         self.c(n).start()
 
-    def c_done(self, n):
+    def c_add(self, n):
         self.c(n).wait_recv()
         self.cr[n] = self.cr[n] + self.g[n, :, rows(self.p.core, self.half), :]
+
+    def c_done(self, n):
+        self.c_add(n)
         self.y(n).start()
+
+    def c_done_x(self, n):
+        self.c_add(n)
+        self.x2(n).start()
+
+    def x2_done(self, n):
+        self.x2(n).wait_recv()
+        r = rows(self.p.x, self.quarter)
+        self.cr[n, :, r, :] = self.cr[n, :, r, :] + self.x2r[n - EARLY]
+        self.y2(n).start()
+
+    def y2_done(self, n):
+        self.y2(n).wait_recv()
+        r = rows(self.p.x, self.quarter)
+        self.cr[n, 0, r, :] = self.cr[n, 0, r, :] + self.y2r[n - EARLY]
+        for copy in self.z(n):
+            copy.start()
 
     def y_done(self, n):
         self.y(n).wait_recv()
@@ -447,37 +495,60 @@
     def ca_done(self, n):
         self.ca(n).wait_recv()
 
-    def drain(self, n):
-        for copy in [self.c(n), self.y(n), self.x(n), self.xa(n), self.ca(n)] + self.z(n) + self.za(n):
+    def drain(self, n, late=False):
+        cross = [self.x2(n), self.y2(n)] if late else [self.x(n), self.y(n)]
+        for copy in cross + [self.c(n), self.xa(n), self.ca(n)] + self.z(n) + self.za(n):
             copy.wait_send()
 
 
 STAGES = ("y_done", "x_done", "z_done", "za_done", "xa_done", "ca_done")
-
-
-def step(big, small, outs, tick):
+STAGES_X = ("x2_done", "y2_done", "z_done", "za_done", "xa_done", "ca_done")
+
+
+def when(condition, body):
+    if isinstance(condition, bool):
+        if condition:
+            body()
+    else:
+        pl.when(condition)(body)
+
+
+def both(a, b):
+    return a and b if isinstance(a, bool) and isinstance(b, bool) else a & b
+
+
+def step(big, outs, tick):
     for lag, name in enumerate(STAGES):
-        unit = tick - lag
-
-        @pl.when((unit >= 0) & (unit < UNITS))
-        def _():
+        unit = tick - LAG * lag
+
+        def run(unit=unit, name=name):
             getattr(big, name)(unit)
             if name == "ca_done":
                 outs(unit).start()
 
-        if small is not None:
-
-            @pl.when(unit == UNITS)
-            def _():
-                getattr(small, name)(0)
+        when(both(unit >= 0, unit < EARLY), run)
+
+
+def step_x(big, small, outs, tick):
+    for lag, name in enumerate(STAGES_X):
+        unit = tick - LAG * lag + EARLY
+
+        def run(unit=unit, name=name):
+            getattr(big, name)(unit)
+            if name == "ca_done":
+                outs(unit).start()
+
+        when(both(unit >= EARLY, unit < UNITS), run)
+        when(unit == UNITS, lambda lag=lag: getattr(small, STAGES[lag])(0))
 
 
 def kernel(caps, slots, pad, names_in, *all_refs):
     L = Layer(caps, slots, pad, dict(zip(names_in, all_refs)))
     peers = Peers()
+    peers.greet()
     L.cap_base = peers.t * caps
     weights = Weights(peers, L.w, L.wsend, L.wrecv)
-    big = Reduce(peers, (L.grads, L.cr, L.yr, L.xr, L.zr, L.f), 0, L.gsend, L.grecv)
+    big = Reduce(peers, (L.grads, L.cr, L.yr, L.xr, L.zr, L.f), 0, L.gsend, L.grecv, (L.x2r, L.y2r))
     small = Reduce(peers, (L.sg, L.scr, L.syr, L.sxr, L.szr, L.sf), UNITS, L.gsend, L.grecv)
 
     local = []
@@ -487,17 +558,21 @@
         copy.start()
         local.append(copy)
 
+    load(L.tok, L.tok_v)
     for j in range(3):
         load(L.wqkv_a.at[j], L.w.at[j])
     for n in range(2):
         load(L.wo_a.at[:, pl.ds(n * 256, 256)], L.w.at[3, pl.ds(n * 256, 256)])
-    load(L.tok, L.tok_v)
     for n in range(4):
         load(L.wu_a.at[:, pl.ds(n * 256, 256)], L.w.at[4 + n])
     for n in range(4):
         for k in range(2):
             load(L.wd_a.at[pl.ds(n * 256, 256), pl.ds(k * 256, 256)], L.w.at[8 + n, pl.ds(k * 256, 256)])
     load(L.cot, L.cot_v)
+    local[0].wait()
+    L.widen(L.tok_v, peers.t * caps * slots, L.xs)
+    for copy in local[1:]:
+        copy.wait()
     peers.meet()
     bias_send = [
         remote(L.qvb, L.qvb_b, L.bsem.at[0], L.bsem.at[1], peers.to_y),
@@ -505,72 +580,48 @@
     ]
     for copy in bias_send:
         copy.start()
-    for copy in local:
-        copy.wait()
     loop(UNITS, lambda u: weights.y(u).start())
-    L.widen(L.tok_v, peers.t * caps * slots, L.xs)
     L.norm_one()
+    L.biases(0, L.qvb, L.ub)
+    loop(3, L.qkv)
+    attend = lambda i: [L.attention(4 * i + k) for k in range(4)]
+    loop(caps // 4, attend)
+    L.widen(L.cot_v, peers.t * caps * slots, L.g)
     for copy in bias_send:
         copy.wait()
-    for s, (qvb, ub) in enumerate(((L.qvb, L.ub), (L.qvb_b, L.ub_b))):
-        for j in range(3):
-            if j == 1:
-                L.bias_qkv[s * 3 + j] = jnp.zeros((1, 256), F32)
-            else:
-                L.bias_qkv[s * 3 + j] = qvb[j // 2 : j // 2 + 1, :].astype(F32)
-        for n in range(4):
-            L.bias_up[s * 4 + n] = ub[:, n * 256 : (n + 1) * 256].astype(F32)
-    loop(3, L.qkv)
-    loop(2, weights.relay_x)
-
-    def attend_own(i):
-        L.attention(i)
-
-        @pl.when(i < 7)
-        def _():
-            weights.relay_x(2 + i)
-
-        @pl.when(i < 8)
-        def _():
-            weights.relay_c(i)
-
-    loop(caps, attend_own)
-    L.widen(L.cot_v, peers.t * caps * slots, L.g)
-    loop(3, lambda i: (weights.ready(i), L.qkv(3 + i)))
-
-    def attend_other(i):
-        L.attention(caps + i)
-
-        @pl.when(i < 3)
-        def _():
-            weights.relay_x(9 + i)
-
-        @pl.when(i < 4)
-        def _():
-            weights.relay_c(8 + i)
-
-    loop(caps, attend_other)
+    L.biases(1, L.qvb_b, L.ub_b)
+    for u in range(3):
+        weights.tick(u)
+    for j in range(3):
+        weights.ready(j)
+        L.qkv(3 + j)
+        weights.tick(3 + j)
+    attend(caps // 4)
+    weights.tick(6)
+    attend(caps // 4 + 1)
+    weights.tick(7)
     weights.ready(3)
     loop(4, L.project)
-    loop(4, L.up)
-    loop(4, lambda i: (weights.ready(4 + i), L.up(4 + i)))
-
-    def down(i):
-        L.down_grad(i)
-        L.down_grad(4 + i)
-        big.c_start(i)
-
-        @pl.when(i > 0)
-        def _():
-            big.c_done(i - 1)
-
-    loop(4, down)
+    weights.tick(8)
+
+    for n in range(4):
+        L.up(n)
+        weights.ready(4 + n)
+        L.up(4 + n)
+        L.down_grad(n)
+        L.down_grad(4 + n)
+        big.c_start(n)
+        if n > 0:
+            big.c_done(n - 1)
+        weights.tick(9 + n)
     loop(4, L.hidden_back)
     big.c_done(3)
+    weights.tick(13)
     loop(4, lambda i: (weights.ready(8 + i), L.hidden_back(4 + i)))
 
     outs = lambda n: pltpu.make_async_copy(L.f.at[n], L.f_out.at[n], L.osem.at[n])
-    tick = functools.partial(step, big, None, outs)
+    tick = functools.partial(step, big, outs)
+    tick(0)
 
     def ups(i):
         L.up_grad(i)
@@ -581,45 +632,33 @@
         def _():
             big.c_done(3 + i)
 
-        @pl.when(lax.rem(i, 2) == 1)
-        def _():
-            tick(i // 2)
-
     loop(4, ups)
+    tick(1)
     loop(4, L.second_grad)
     big.c_done(7)
+    L.norm_two_back()
     tick(2)
-    L.norm_two_back()
     loop(2, L.out_back)
     big.c_start(8)
-    tick(3)
 
     def attend_back(i):
-        L.attention_back(i)
-
-        @pl.when(i == 1)
-        def _():
-            big.c_done(8)
-
-        @pl.when(lax.rem(i, 6) == 5)
-        def _():
-            tick(4 + i // 6)
-
-    loop(2 * caps, attend_back)
+        for k in range(4):
+            L.attention_back(4 * i + k)
+        when(i == 0, lambda: big.c_done(8))
+        when(lax.rem(i, 2) == 1, lambda: tick(3 + i // 2))
+
+    loop(caps // 2, attend_back)
 
     def qkvs(i):
         L.qkv_grad(i)
         L.qkv_grad(3 + i)
         big.c_start(9 + i)
-
-        @pl.when(i > 0)
-        def _():
-            big.c_done(8 + i)
+        when(i > 0, lambda: big.c_done_x(8 + i))
 
     loop(3, qkvs)
-    tick(6)
     loop(4, L.first_grad)
-    big.c_done(11)
+    big.c_done_x(11)
+    tick(5)
     size = caps * slots
     base = (size + 7) // 8 * 8
     L.norm_one_back(L.stage, base)
@@ -627,35 +666,43 @@
     dx_copy.start()
     L.pack_small(L.sg.at[0])
     small.c_start(0)
-    tick(7)
     loop(4, L.mlp_out)
+    tick(6)
     L.layer_out(L.stage, L.yb)
     y_copy = pltpu.make_async_copy(L.yb, L.y_out, L.osem.at[UNITS + 1])
     y_copy.start()
     small.c_done(0)
-    loop(UNITS + len(STAGES) - 8, lambda i: step(big, small, outs, 8 + i))
+    late = UNITS - EARLY
+
+    def last(i):
+        step(big, outs, 7 + i)
+        step_x(big, small, outs, i)
+
+    loop(max(EARLY + LAG * (len(STAGES) - 1) - 7, late + 1 + LAG * (len(STAGES) - 1)), last)
     s_copy = pltpu.make_async_copy(L.sf.at[0], L.s_out, L.osem.at[UNITS + 2])
     s_copy.start()
 
     def drain(n):
         weights.drain(n)
-        big.drain(n)
         outs(n).wait()
 
     loop(UNITS, drain)
+    loop(EARLY, big.drain)
+    loop(late, lambda i: big.drain(EARLY + i, late=True))
     small.drain(0)
     dx_copy.wait()
     y_copy.wait()
     s_copy.wait()
 
 
-def finish(f, s, y, dx, y_out, dx_out, qkv, out, up, down, qvb, ob, ub, db, gg, sh, f_v, wide, sem_in, sem_out, sem_io):
+def finish(f, s, y, dx, y_out, dx_out, qkv, out, up, down, qvb, ob, ub, db, gg, sh, f_v, y_v, dx_v, wide, sem_in, sem_out, sem_io):
     ins = [pltpu.make_async_copy(f.at[n], f_v.at[n], sem_in.at[n]) for n in range(UNITS)]
     for copy in ins:
         copy.start()
-    io = [pltpu.make_async_copy(y, y_out, sem_io.at[0]), pltpu.make_async_copy(dx, dx_out, sem_io.at[1])]
-    for copy in io:
+    rows_in = [pltpu.make_async_copy(y, y_v, sem_io.at[0]), pltpu.make_async_copy(dx, dx_v, sem_io.at[1])]
+    for copy in rows_in:
         copy.start()
+    io = []
     for n in range(UNITS):
         ins[n].wait()
         wide[n] = f_v[n].astype(F32)
@@ -673,6 +720,13 @@
             copy = pltpu.make_async_copy(a, b, sem_out.at[2 * n + k])
             copy.start()
             io.append(copy)
+        if n == 3:
+            for copy in rows_in:
+                copy.wait()
+            for k, (a, b) in enumerate(((y_v, y_out), (dx_v, dx_out))):
+                copy = pltpu.make_async_copy(a, b, sem_io.at[2 + k])
+                copy.start()
+                io.append(copy)
 
     def row(first, count):
         return jnp.concatenate([s[first + i : first + i + 1, :] for i in range(count)], axis=1)
@@ -699,8 +753,8 @@
     ins = [
         ("tok", tokens, A), ("cot", cotangent, A), ("lengths", lengths, S),
         ("wqkv_a", qkv_weight, A), ("wo_a", out_weight, A), ("wu_a", up_weight, A), ("wd_a", down_weight, A),
-        ("qvb", qv_bias, V), ("ub", up_bias[None], V),
-        ("ob", out_bias[None], V), ("db", down_bias[None], V), ("gains", norm_gain, V), ("shifts", norm_shift, V),
+        ("qvb", qv_bias, V), ("ub", up_bias, V),
+        ("ob", out_bias, V), ("db", down_bias, V), ("gains", norm_gain, V), ("shifts", norm_shift, V),
     ]
     outs = [
         ("y_out", (caps * slots, 512), BF16), ("dx_out", (caps * slots, 512), F32),
@@ -712,7 +766,7 @@
         ("tok_v", vm((total, 512), BF16)), ("cot_v", vm((total, 512), BF16)),
         ("stage", vm((total + 16, 512), F32)), ("xs", vm((rws, 512), BF16)), ("g", vm((rws, 512), BF16)),
         ("n1", vm((rws, 512), F32)), ("r1", vm((rws, 128), F32)), ("a1", vm((rws, 512), BF16)),
-        ("w", vm((2 * UNITS, 512, 256), BF16)), ("qvb_b", vm((2, 256), BF16)), ("ub_b", vm((1, 1024), BF16)),
+        ("w", vm((2 * UNITS, 512, 256), BF16)), ("qvb_b", vm((2, 256), BF16)), ("ub_b", vm(up_bias.shape, BF16)),
         ("bias_qkv", vm((6, 1, 256), F32)), ("bias_up", vm((8, 1, 256), F32)),
         ("pqkv", vm((6, rws, 256), BF16)), ("probs", vm((2 * caps, 4 * pad, pad), F32)), ("ctx", vm((2, rws, 256), BF16)),
         ("h1", vm((rws, 512), F32)), ("n2", vm((rws, 512), F32)), ("r2", vm((rws, 128), F32)), ("a2", vm((rws, 512), BF16)),
@@ -722,6 +776,7 @@
         ("small", vm((8, 512), F32)), ("small_up", vm((8, 1, 256), F32)), ("small_qkv", vm((6, 1, 256), F32)),
         ("grads", vm((UNITS, 2, 512, 256), BF16)), ("cr", vm((UNITS, 2, 256, 256), BF16)), ("yr", vm((UNITS, 256, 256), BF16)),
         ("xr", vm((UNITS, 128, 256), BF16)), ("zr", vm((UNITS, depth - 1, 128 // depth, 256), BF16)), ("f", vm((UNITS, 512, 256), BF16)),
+        ("x2r", vm((UNITS - EARLY, 2, 128, 256), BF16)), ("y2r", vm((UNITS - EARLY, 128, 256), BF16)),
         ("sg", vm((1, 2, 128, 128), F32)), ("scr", vm((1, 2, 64, 128), F32)), ("syr", vm((1, 64, 128), F32)),
         ("sxr", vm((1, 32, 128), F32)), ("szr", vm((1, depth - 1, 32 // depth, 128), F32)), ("sf", vm((1, 128, 128), F32)),
         ("lsem", pltpu.SemaphoreType.DMA((20,))), ("osem", pltpu.SemaphoreType.DMA((UNITS + 3,))), ("bsem", pltpu.SemaphoreType.DMA((4,))),
@@ -749,10 +804,10 @@
         in_specs=[A, V, A, A],
         out_specs=[s for _, _, s in results],
         scratch_shapes=[
-            vm((UNITS, 512, 256), BF16), vm((UNITS, 512, 256), F32),
-            pltpu.SemaphoreType.DMA((UNITS,)), pltpu.SemaphoreType.DMA((2 * UNITS,)), pltpu.SemaphoreType.DMA((2,)),
+            vm((UNITS, 512, 256), BF16), vm(y.shape, BF16), vm(dx.shape, F32), vm((UNITS, 512, 256), F32),
+            pltpu.SemaphoreType.DMA((UNITS,)), pltpu.SemaphoreType.DMA((2 * UNITS,)), pltpu.SemaphoreType.DMA((4,)),
         ],
-        compiler_params=pltpu.CompilerParams(vmem_limit_bytes=24 << 20),
+        compiler_params=pltpu.CompilerParams(vmem_limit_bytes=61 << 20),
         name="finish",
     )(f, s, y, dx)
     return y, dx, qkv, qvb, out, ob[0], up, ub[0], down, db[0], gg, sh

time: 124 us -> 108 us (0.87)
  local copies, waits for them, and re-layouts: 8.89 us -> 0 us
  Pallas kernels: 114 us -> 106 us
    pallas_call x1, Pallas kernels: 109 us -> 98.9 us  [shards(): pl.pallas_call(functools.partial(kernel, caps, slots, pad, names), out_sh...]
    unnamed x8 -> x0, local copies, waits for them, and re-layouts: 5.1 us -> none
    broadcast_in_dim x3 -> x0, local copies, waits for them, and re-layouts: 3.8 us -> none  [the longest x1 1.28 us: shards(): up_bias[None]]
    pallas_call x1, Pallas kernels: 4.38 us -> 7.59 us  [shards(): pl.pallas_call(finish, out_shape=[jax.ShapeDtypeStruct(s, d) for s, d, _...]
where the time goes in v2:
time: 108 us; the launch traced here: 107 us
  Pallas kernels  106 us (98%)
    pallas_call x1, Pallas kernels, shards(): pl.pallas_call(functools.partial(kernel, caps, slots, pad, names), out_sh...  98.9 us
    pallas_call x1, Pallas kernels, shards(): pl.pallas_call(finish, out_shape=[jax.ShapeDtypeStruct(s, d) for s, d, _...  7.59 us

profile of v2, /device:TPU:0, one launch (start us, length us, event | category | flops | bytes accessed | tf_op | source)
XLA Modules:
  0.0 107.3 jit_solution(3354490372388088565)
XLA Ops:
  0.6 98.9 %layer.1 = (bf16[616,512]{1,0:T(8,128)(2,1)}, f32[616,512]{1,0:T(8,128)}, bf16[12,512,256]{2,1,0:T(8,128)(2,1)}, f32[128,128]{1,0:T(8,128)}) custom-call(bf16[1232,512]{1,0:T(8,128)(2,1)} %all_refs_0_.1, bf16[1232,512]{1,0:T(8,128)(2,1)} %all_refs_1_.1, s32[16]{0:T(128)} %all_refs_2_.1, bf16[3,512,256]{2,1,0:T(8,128)(2,1)} %all_refs_3_.1, ...), custom_call_target="tpu_custom_call" | custom-call | tf_op jit(solution)/shard_map/layer/pallas_call | solution.py:787
  99.6 7.6 %finish.1 = (bf16[616,512]{1,0:T(8,128)(2,1)}, f32[616,512]{1,0:T(8,128)}, f32[3,512,256]{2,1,0:T(8,128)}, f32[256,512]{1,0:T(8,128)}, f32[512,1024]{1,0:T(8,128...) custom-call(bf16[12,512,256]{2,1,0:T(8,128)(2,1)} %get-tuple-element, ...), custom_call_target="tpu_custom_call" | custom-call | tf_op jit(solution)/shard_map/finish/pallas_call | solution.py:801

commit v3 on v2

--- a/solution.py
+++ b/solution.py
@@ -13,8 +13,6 @@
 BF16 = jnp.bfloat16
 LOG2E = 1.4426950408889634
 UNITS = 12
-EARLY = 9
-LAG = 2
 MESH = pl.DeviceIdType.MESH
 
 
@@ -357,12 +355,6 @@
         self.x(u).wait_recv()
         self.c(u).start()
 
-    def tick(self, u):
-        if u < UNITS:
-            self.relay_x(u)
-        if 2 <= u < UNITS + 2:
-            self.relay_c(u - 2)
-
     def ready(self, u):
         self.c(u).wait_recv()
 
@@ -373,10 +365,9 @@
 
 
 class Reduce:
-    def __init__(self, peers, refs, sem0, send, recv, across=None):
+    def __init__(self, peers, refs, sem0, send, recv):
         self.p = peers
         self.g, self.cr, self.yr, self.xr, self.zr, self.f = refs
-        self.x2r, self.y2r = across or (None, None)
         self.sem0, self.send, self.recv = sem0, send, recv
         self.count = self.g.shape[0]
         self.full = self.g.shape[2]
@@ -394,14 +385,6 @@
 
     def x(self, n):
         return remote(self.cr.at[n, 0, rows(1 - self.p.x, self.quarter)], self.xr.at[n], *self.sems(n, 2), self.p.to_x)
-
-    def x2(self, n):
-        return remote(
-            self.cr.at[n, :, rows(1 - self.p.x, self.quarter)], self.x2r.at[n - EARLY], *self.sems(n, 2), self.p.to_x
-        )
-
-    def y2(self, n):
-        return remote(self.cr.at[n, 1, rows(self.p.x, self.quarter)], self.y2r.at[n - EARLY], *self.sems(n, 1), self.p.to_y)
 
     def z(self, n):
         return [
@@ -435,30 +418,10 @@
     def c_start(self, n):
         self.c(n).start()
 
-    def c_add(self, n):
+    def c_done(self, n):
         self.c(n).wait_recv()
         self.cr[n] = self.cr[n] + self.g[n, :, rows(self.p.core, self.half), :]
-
-    def c_done(self, n):
-        self.c_add(n)
         self.y(n).start()
-
-    def c_done_x(self, n):
-        self.c_add(n)
-        self.x2(n).start()
-
-    def x2_done(self, n):
-        self.x2(n).wait_recv()
-        r = rows(self.p.x, self.quarter)
-        self.cr[n, :, r, :] = self.cr[n, :, r, :] + self.x2r[n - EARLY]
-        self.y2(n).start()
-
-    def y2_done(self, n):
-        self.y2(n).wait_recv()
-        r = rows(self.p.x, self.quarter)
-        self.cr[n, 0, r, :] = self.cr[n, 0, r, :] + self.y2r[n - EARLY]
-        for copy in self.z(n):
-            copy.start()
 
     def y_done(self, n):
         self.y(n).wait_recv()
@@ -495,14 +458,9 @@
     def ca_done(self, n):
         self.ca(n).wait_recv()
 
-    def drain(self, n, late=False):
-        cross = [self.x2(n), self.y2(n)] if late else [self.x(n), self.y(n)]
-        for copy in cross + [self.c(n), self.xa(n), self.ca(n)] + self.z(n) + self.za(n):
+    def drain(self, n):
+        for copy in [self.c(n), self.y(n), self.x(n), self.xa(n), self.ca(n)] + self.z(n) + self.za(n):
             copy.wait_send()
-
-
-STAGES = ("y_done", "x_done", "z_done", "za_done", "xa_done", "ca_done")
-STAGES_X = ("x2_done", "y2_done", "z_done", "za_done", "xa_done", "ca_done")
 
 
 def when(condition, body):
@@ -513,33 +471,29 @@
         pl.when(condition)(body)
 
 
-def both(a, b):
-    return a and b if isinstance(a, bool) and isinstance(b, bool) else a & b
-
-
-def step(big, outs, tick):
-    for lag, name in enumerate(STAGES):
-        unit = tick - LAG * lag
-
-        def run(unit=unit, name=name):
-            getattr(big, name)(unit)
-            if name == "ca_done":
-                outs(unit).start()
-
-        when(both(unit >= 0, unit < EARLY), run)
-
-
-def step_x(big, small, outs, tick):
-    for lag, name in enumerate(STAGES_X):
-        unit = tick - LAG * lag + EARLY
-
-        def run(unit=unit, name=name):
-            getattr(big, name)(unit)
-            if name == "ca_done":
-                outs(unit).start()
-
-        when(both(unit >= EARLY, unit < UNITS), run)
-        when(unit == UNITS, lambda lag=lag: getattr(small, STAGES[lag])(0))
+ON_WEIGHTS = ("relay_x", "relay_c", "ready")
+ON_GRADS = ("c_start", "c_done", "y_done", "x_done", "z_done", "za_done", "xa_done", "ca_done")
+PLAN = {
+    "norm_one": (),
+    "qkv_own": (),
+    "att_own": ((1, 0, (0,)), ),
+    "widen_g": ((0, 0, (1,)), ),
+    "qkv_other": ((0, 0, (2, 100, 3, 200,)), (1, 0, (101, 4, 201,)), (2, 0, (102, 5, 202,)), ),
+    "att_other": ((0, 0, (103,)), (1, 0, (104, 6,)), ),
+    "proj": ((0, 0, (105, 7, 8, 203,)), ),
+    "updown": ((0, 0, (9, 106,)), (0, 1, (204,)), (0, 3, (10,)), (1, 0, (1000, 107,)), (1, 1, (205,)), (1, 2, (11,)), (1, 3, (108, 1100,)), (2, 0, (1001,)), (2, 1, (206,)), (2, 2, (109,)), (2, 3, (1101,)), (3, 0, (1002,)), (3, 1, (110, 207,)), ),
+    "hbug": ((0, 0, (1003, 111, 1102,)), (0, 1, (1200, 208,)), (1, 0, (1004,)), (1, 1, (209,)), (1, 2, (1103,)), (1, 3, (1201,)), (2, 0, (1005, 1300,)), (2, 1, (210,)), (3, 0, (1006, 1202, 1104,)), (3, 1, (211,)), (3, 2, (1301,)), ),
+    "sg": ((0, 0, (1007, 1400,)), (1, 0, (1105, 1203,)), (2, 0, (1302,)), ),
+    "ntb": (),
+    "ob": ((0, 0, (1401, 1204, 1303, 1500, 1106,)), ),
+    "ab": ((0, 0, (1008,)), (1, 0, (1402, 1205, 1107,)), (2, 0, (1501, 1304,)), (3, 0, (1600, 1403, 1206, 1108,)), ),
+    "qg": ((0, 0, (1700, 1502, 1305,)), (1, 0, (1009, 1601, 1404, 1207,)), (2, 0, (1010, 1306, 1109, 1503,)), (2, 1, (1701,)), ),
+    "fg": ((0, 0, (1011,)), (1, 0, (1602, 1208, 1405, 1110,)), (3, 0, (1702, 1307,)), ),
+    "nob": ((0, 0, (1504,)), ),
+    "mo": ((0, 0, (1012, 1603,)), (1, 0, (1406, 1209, 1111,)), (2, 0, (1703, 1308,)), (3, 0, (1505,)), ),
+    "lo": (),
+    "tail": ((0, 0, (1604, 1112, 1407, 1210, 1704, 1309, 1506, 1605, 1408, 1211, 1705, 1212, 1310, 1507, 1606, 1409, 1706, 1311, 1508, 1312, 1607, 1410, 1707, 1509, 1608, 1411, 1708, 1412, 1510, 1609, 1709, 1511, 1512, 1610, 1710, 1611, 1612, 1711, 1712,)), ),
+}
 
 
 def kernel(caps, slots, pad, names_in, *all_refs):
@@ -548,8 +502,34 @@
     peers.greet()
     L.cap_base = peers.t * caps
     weights = Weights(peers, L.w, L.wsend, L.wrecv)
-    big = Reduce(peers, (L.grads, L.cr, L.yr, L.xr, L.zr, L.f), 0, L.gsend, L.grecv, (L.x2r, L.y2r))
+    big = Reduce(peers, (L.grads, L.cr, L.yr, L.xr, L.zr, L.f), 0, L.gsend, L.grecv)
     small = Reduce(peers, (L.sg, L.scr, L.syr, L.sxr, L.szr, L.sf), UNITS, L.gsend, L.grecv)
+    outs = lambda n: pltpu.make_async_copy(L.f.at[n], L.f_out.at[n], L.osem.at[n])
+
+    def arrive(codes):
+        for code in codes:
+            stage, unit = code // 100, code % 100
+            if stage < 10:
+                getattr(weights, ON_WEIGHTS[stage])(unit)
+            elif unit == UNITS:
+                getattr(small, ON_GRADS[stage - 10])(0)
+            else:
+                getattr(big, ON_GRADS[stage - 10])(unit)
+                if stage == 17:
+                    outs(unit).start()
+
+    def run(name, count, *parts):
+        def body(i):
+            for k, part in enumerate(parts):
+                for when_i, when_k, codes in PLAN[name]:
+                    if when_k == k:
+                        when(i == when_i, functools.partial(arrive, codes))
+                part(i)
+
+        if count == 1:
+            body(0)
+        else:
+            loop(count, body)
 
     local = []
 
@@ -581,114 +561,55 @@
     for copy in bias_send:
         copy.start()
     loop(UNITS, lambda u: weights.y(u).start())
-    L.norm_one()
-    L.biases(0, L.qvb, L.ub)
-    loop(3, L.qkv)
     attend = lambda i: [L.attention(4 * i + k) for k in range(4)]
-    loop(caps // 4, attend)
-    L.widen(L.cot_v, peers.t * caps * slots, L.g)
-    for copy in bias_send:
-        copy.wait()
-    L.biases(1, L.qvb_b, L.ub_b)
-    for u in range(3):
-        weights.tick(u)
-    for j in range(3):
-        weights.ready(j)
-        L.qkv(3 + j)
-        weights.tick(3 + j)
-    attend(caps // 4)
-    weights.tick(6)
-    attend(caps // 4 + 1)
-    weights.tick(7)
-    weights.ready(3)
-    loop(4, L.project)
-    weights.tick(8)
-
-    for n in range(4):
-        L.up(n)
-        weights.ready(4 + n)
-        L.up(4 + n)
-        L.down_grad(n)
-        L.down_grad(4 + n)
-        big.c_start(n)
-        if n > 0:
-            big.c_done(n - 1)
-        weights.tick(9 + n)
-    loop(4, L.hidden_back)
-    big.c_done(3)
-    weights.tick(13)
-    loop(4, lambda i: (weights.ready(8 + i), L.hidden_back(4 + i)))
-
-    outs = lambda n: pltpu.make_async_copy(L.f.at[n], L.f_out.at[n], L.osem.at[n])
-    tick = functools.partial(step, big, outs)
-    tick(0)
-
-    def ups(i):
-        L.up_grad(i)
-        L.up_grad(4 + i)
-        big.c_start(4 + i)
-
-        @pl.when(i > 0)
-        def _():
-            big.c_done(3 + i)
-
-    loop(4, ups)
-    tick(1)
-    loop(4, L.second_grad)
-    big.c_done(7)
-    L.norm_two_back()
-    tick(2)
-    loop(2, L.out_back)
-    big.c_start(8)
-
-    def attend_back(i):
-        for k in range(4):
-            L.attention_back(4 * i + k)
-        when(i == 0, lambda: big.c_done(8))
-        when(lax.rem(i, 2) == 1, lambda: tick(3 + i // 2))
-
-    loop(caps // 2, attend_back)
-
-    def qkvs(i):
-        L.qkv_grad(i)
-        L.qkv_grad(3 + i)
-        big.c_start(9 + i)
-        when(i > 0, lambda: big.c_done_x(8 + i))
-
-    loop(3, qkvs)
-    loop(4, L.first_grad)
-    big.c_done_x(11)
-    tick(5)
+
+    def rows_and_biases():
+        L.widen(L.cot_v, peers.t * caps * slots, L.g)
+        for copy in bias_send:
+            copy.wait()
+        L.biases(1, L.qvb_b, L.ub_b)
+
     size = caps * slots
     base = (size + 7) // 8 * 8
-    L.norm_one_back(L.stage, base)
     dx_copy = pltpu.make_async_copy(L.stage.at[pl.ds(base, size)], L.dx_out, L.osem.at[UNITS])
-    dx_copy.start()
-    L.pack_small(L.sg.at[0])
-    small.c_start(0)
-    loop(4, L.mlp_out)
-    tick(6)
-    L.layer_out(L.stage, L.yb)
     y_copy = pltpu.make_async_copy(L.yb, L.y_out, L.osem.at[UNITS + 1])
-    y_copy.start()
-    small.c_done(0)
-    late = UNITS - EARLY
-
-    def last(i):
-        step(big, outs, 7 + i)
-        step_x(big, small, outs, i)
-
-    loop(max(EARLY + LAG * (len(STAGES) - 1) - 7, late + 1 + LAG * (len(STAGES) - 1)), last)
     s_copy = pltpu.make_async_copy(L.sf.at[0], L.s_out, L.osem.at[UNITS + 2])
-    s_copy.start()
+
+    def input_rows():
+        L.norm_one_back(L.stage, base)
+        dx_copy.start()
+        L.pack_small(L.sg.at[0])
+
+    def output_rows():
+        L.layer_out(L.stage, L.yb)
+        y_copy.start()
+
+    run("norm_one", 1, lambda i: (L.norm_one(), L.biases(0, L.qvb, L.ub)))
+    run("qkv_own", 3, L.qkv)
+    run("att_own", caps // 4, attend)
+    run("widen_g", 1, lambda i: rows_and_biases())
+    run("qkv_other", 3, lambda j: L.qkv(3 + j))
+    run("att_other", caps // 4, lambda i: attend(caps // 4 + i))
+    run("proj", 4, L.project)
+    run("updown", 4, L.up, lambda n: L.up(4 + n), L.down_grad, lambda n: L.down_grad(4 + n))
+    run("hbug", 4, L.hidden_back, lambda n: L.hidden_back(4 + n), L.up_grad, lambda n: L.up_grad(4 + n))
+    run("sg", 4, L.second_grad)
+    run("ntb", 1, lambda i: L.norm_two_back())
+    run("ob", 2, L.out_back)
+    run("ab", caps // 2, lambda i: [L.attention_back(4 * i + k) for k in range(4)])
+    run("qg", 3, L.qkv_grad, lambda j: L.qkv_grad(3 + j))
+    run("fg", 4, L.first_grad)
+    run("nob", 1, lambda i: input_rows())
+    run("mo", 4, L.mlp_out)
+    run("lo", 1, lambda i: output_rows())
+    run("tail", 1, lambda i: s_copy.start())
 
     def drain(n):
         weights.drain(n)
+        big.drain(n)
         outs(n).wait()
 
     loop(UNITS, drain)
-    loop(EARLY, big.drain)
-    loop(late, lambda i: big.drain(EARLY + i, late=True))
     small.drain(0)
     dx_copy.wait()
     y_copy.wait()
@@ -776,7 +697,6 @@
         ("small", vm((8, 512), F32)), ("small_up", vm((8, 1, 256), F32)), ("small_qkv", vm((6, 1, 256), F32)),
         ("grads", vm((UNITS, 2, 512, 256), BF16)), ("cr", vm((UNITS, 2, 256, 256), BF16)), ("yr", vm((UNITS, 256, 256), BF16)),
         ("xr", vm((UNITS, 128, 256), BF16)), ("zr", vm((UNITS, depth - 1, 128 // depth, 256), BF16)), ("f", vm((UNITS, 512, 256), BF16)),
-        ("x2r", vm((UNITS - EARLY, 2, 128, 256), BF16)), ("y2r", vm((UNITS - EARLY, 128, 256), BF16)),
         ("sg", vm((1, 2, 128, 128), F32)), ("scr", vm((1, 2, 64, 128), F32)), ("syr", vm((1, 64, 128), F32)),
         ("sxr", vm((1, 32, 128), F32)), ("szr", vm((1, depth - 1, 32 // depth, 128), F32)), ("sf", vm((1, 128, 128), F32)),
         ("lsem", pltpu.SemaphoreType.DMA((20,))), ("osem", pltpu.SemaphoreType.DMA((UNITS + 3,))), ("bsem", pltpu.SemaphoreType.DMA((4,))),

time: 108 us -> 95.3 us (0.88)
  Pallas kernels: 106 us -> 93.8 us
    pallas_call x1, Pallas kernels: 98.9 us -> 86.2 us  [shards(): pl.pallas_call(functools.partial(kernel, caps, slots, pad, names), out_sh...]
where the time goes in v3:
time: 95.3 us; the launch traced here: 94.5 us
  Pallas kernels  93.8 us (98%)
    pallas_call x1, Pallas kernels, shards(): pl.pallas_call(functools.partial(kernel, caps, slots, pad, names), out_sh...  86.2 us
    pallas_call x1, Pallas kernels, shards(): pl.pallas_call(finish, out_shape=[jax.ShapeDtypeStruct(s, d) for s, d, _...  7.59 us

profile of v3, /device:TPU:0, one launch (start us, length us, event | category | flops | bytes accessed | tf_op | source)
XLA Modules:
  0.0 94.5 jit_solution(11712558190317635187)
XLA Ops:
  0.6 86.2 %layer.1 = (bf16[616,512]{1,0:T(8,128)(2,1)}, f32[616,512]{1,0:T(8,128)}, bf16[12,512,256]{2,1,0:T(8,128)(2,1)}, f32[128,128]{1,0:T(8,128)}) custom-call(bf16[1232,512]{1,0:T(8,128)(2,1)} %all_refs_0_.1, bf16[1232,512]{1,0:T(8,128)(2,1)} %all_refs_1_.1, s32[16]{0:T(128)} %all_refs_2_.1, bf16[3,512,256]{2,1,0:T(8,128)(2,1)} %all_refs_3_.1, ...), custom_call_target="tpu_custom_call" | custom-call | tf_op jit(solution)/shard_map/layer/pallas_call | solution.py:707
  86.9 7.6 %finish.1 = (bf16[616,512]{1,0:T(8,128)(2,1)}, f32[616,512]{1,0:T(8,128)}, f32[3,512,256]{2,1,0:T(8,128)}, f32[256,512]{1,0:T(8,128)}, f32[512,1024]{1,0:T(8,128...) custom-call(bf16[12,512,256]{2,1,0:T(8,128)(2,1)} %get-tuple-element, ...), custom_call_target="tpu_custom_call" | custom-call | tf_op jit(solution)/shard_map/finish/pallas_call | solution.py:721

commit v4 on v3

--- a/solution.py
+++ b/solution.py
@@ -13,6 +13,7 @@
 BF16 = jnp.bfloat16
 LOG2E = 1.4426950408889634
 UNITS = 12
+VLIM = 54 << 20
 MESH = pl.DeviceIdType.MESH
 
 
@@ -144,7 +145,7 @@
         q = self.pqkv[s * 3, r, :]
         k = self.pqkv[s * 3 + 1, r, :]
         v = self.pqkv[s * 3 + 2, r, :]
-        d = self.dctx[s, r, :]
+        d = self.ctx[s, r, :]
         p = self.probs[i]
         self.dqkv[s * 3 + 2, r, :] = self.unstack(nn(p.astype(BF16), d)).astype(BF16)
         dp = nt(self.stack(v), d)
@@ -233,7 +234,7 @@
             r = self.crows(c)
             e, n, g = self.e[r, :], self.n2[r, :], self.g[r, :].astype(F32)
             dh = g + norm_back(e, n, self.r2[r, 0:1], gain)
-            self.dh1[r, :] = dh
+            self.n2[r, :] = dh
             dob = dh.astype(BF16)
             self.dob[r, :] = dob
             return (gg + colsum(e * n), sg + colsum(e), ob + colsum(dob.astype(F32)), db + colsum(g))
@@ -246,7 +247,7 @@
         self.grads[8, s, 256:512, :] = w[:, 256:]
         wo = s * UNITS + 3
         back = nt(self.dob[:, 0:256], self.w[wo, 0:256, :]) + nt(self.dob[:, 256:512], self.w[wo, 256:512, :])
-        self.dctx[s] = back.astype(BF16)
+        self.ctx[s] = back.astype(BF16)
 
     def qkv_grad(self, i):
         s, j = i // 3, lax.rem(i, 3)
@@ -263,15 +264,15 @@
             acc = part if acc is None else acc + part
         self.e[r, w] = acc
 
-    def norm_one_back(self, out, base):
+    def norm_one_back(self, out):
         gain = self.gains[0:1, :].astype(F32)
         zero = jnp.zeros((1, gain.shape[1]), F32)
         gg, sg = zero, zero
         for c in range(self.caps):
             r = slice(c * self.pad, (c + 1) * self.pad)
             e, n = self.e[r, :], self.n1[r, :]
-            dx = self.dh1[r, :] + norm_back(e, n, self.r1[r, 0:1], gain)
-            out[base + c * self.slots : base + (c + 1) * self.slots, :] = dx[: self.slots]
+            dx = self.n2[r, :] + norm_back(e, n, self.r1[r, 0:1], gain)
+            out[c * self.slots : (c + 1) * self.slots, :] = dx[: self.slots]
             gg, sg = gg + colsum(e * n), sg + colsum(e)
         self.small[0:1, :], self.small[2:3, :] = gg, sg
 
@@ -504,7 +505,6 @@
     weights = Weights(peers, L.w, L.wsend, L.wrecv)
     big = Reduce(peers, (L.grads, L.cr, L.yr, L.xr, L.zr, L.f), 0, L.gsend, L.grecv)
     small = Reduce(peers, (L.sg, L.scr, L.syr, L.sxr, L.szr, L.sf), UNITS, L.gsend, L.grecv)
-    outs = lambda n: pltpu.make_async_copy(L.f.at[n], L.f_out.at[n], L.osem.at[n])
 
     def arrive(codes):
         for code in codes:
@@ -515,8 +515,6 @@
                 getattr(small, ON_GRADS[stage - 10])(0)
             else:
                 getattr(big, ON_GRADS[stage - 10])(unit)
-                if stage == 17:
-                    outs(unit).start()
 
     def run(name, count, *parts):
         def body(i):
@@ -569,20 +567,12 @@
             copy.wait()
         L.biases(1, L.qvb_b, L.ub_b)
 
-    size = caps * slots
-    base = (size + 7) // 8 * 8
-    dx_copy = pltpu.make_async_copy(L.stage.at[pl.ds(base, size)], L.dx_out, L.osem.at[UNITS])
-    y_copy = pltpu.make_async_copy(L.yb, L.y_out, L.osem.at[UNITS + 1])
-    s_copy = pltpu.make_async_copy(L.sf.at[0], L.s_out, L.osem.at[UNITS + 2])
-
     def input_rows():
-        L.norm_one_back(L.stage, base)
-        dx_copy.start()
+        L.norm_one_back(L.dx_out)
         L.pack_small(L.sg.at[0])
 
     def output_rows():
-        L.layer_out(L.stage, L.yb)
-        y_copy.start()
+        L.layer_out(L.stage, L.y_out)
 
     run("norm_one", 1, lambda i: (L.norm_one(), L.biases(0, L.qvb, L.ub)))
     run("qkv_own", 3, L.qkv)
@@ -602,31 +592,22 @@
     run("nob", 1, lambda i: input_rows())
     run("mo", 4, L.mlp_out)
     run("lo", 1, lambda i: output_rows())
-    run("tail", 1, lambda i: s_copy.start())
+    run("tail", 1, lambda i: None)
 
     def drain(n):
         weights.drain(n)
         big.drain(n)
-        outs(n).wait()
 
     loop(UNITS, drain)
     small.drain(0)
-    dx_copy.wait()
-    y_copy.wait()
-    s_copy.wait()
-
-
-def finish(f, s, y, dx, y_out, dx_out, qkv, out, up, down, qvb, ob, ub, db, gg, sh, f_v, y_v, dx_v, wide, sem_in, sem_out, sem_io):
-    ins = [pltpu.make_async_copy(f.at[n], f_v.at[n], sem_in.at[n]) for n in range(UNITS)]
-    for copy in ins:
+
+
+def finish(f, s, y, dx, y_out, dx_out, qkv, out, up, down, qvb, ob, ub, db, gg, sh, wide, sem_out, sem_io):
+    io = [pltpu.make_async_copy(y, y_out, sem_io.at[0]), pltpu.make_async_copy(dx, dx_out, sem_io.at[1])]
+    for copy in io:
         copy.start()
-    rows_in = [pltpu.make_async_copy(y, y_v, sem_io.at[0]), pltpu.make_async_copy(dx, dx_v, sem_io.at[1])]
-    for copy in rows_in:
-        copy.start()
-    io = []
     for n in range(UNITS):
-        ins[n].wait()
-        wide[n] = f_v[n].astype(F32)
+        wide[n] = f[n].astype(F32)
         if n < 4 or n == 8:
             parts = []
             for k in range(2):
@@ -641,16 +622,9 @@
             copy = pltpu.make_async_copy(a, b, sem_out.at[2 * n + k])
             copy.start()
             io.append(copy)
-        if n == 3:
-            for copy in rows_in:
-                copy.wait()
-            for k, (a, b) in enumerate(((y_v, y_out), (dx_v, dx_out))):
-                copy = pltpu.make_async_copy(a, b, sem_io.at[2 + k])
-                copy.start()
-                io.append(copy)
 
     def row(first, count):
-        return jnp.concatenate([s[first + i : first + i + 1, :] for i in range(count)], axis=1)
+        return jnp.concatenate([s[0, first + i : first + i + 1, :] for i in range(count)], axis=1)
 
     qvb[0:1, :], qvb[1:2, :] = row(0, 2), row(2, 2)
     ub[...] = row(4, 8)
@@ -679,7 +653,7 @@
     ]
     outs = [
         ("y_out", (caps * slots, 512), BF16), ("dx_out", (caps * slots, 512), F32),
-        ("f_out", (UNITS, 512, 256), BF16), ("s_out", (128, 128), F32),
+        ("f", (UNITS, 512, 256), BF16), ("sf", (1, 128, 128), F32),
     ]
     vm = pltpu.VMEM
     sems = UNITS + 1, 3 + 2 * depth
@@ -692,25 +666,25 @@
         ("pqkv", vm((6, rws, 256), BF16)), ("probs", vm((2 * caps, 4 * pad, pad), F32)), ("ctx", vm((2, rws, 256), BF16)),
         ("h1", vm((rws, 512), F32)), ("n2", vm((rws, 512), F32)), ("r2", vm((rws, 128), F32)), ("a2", vm((rws, 512), BF16)),
         ("hid", vm((8, rws, 256), BF16)), ("act", vm((8, rws, 256), F32)), ("du", vm((8, rws, 256), BF16)),
-        ("e", vm((rws, 512), F32)), ("dh1", vm((rws, 512), F32)), ("dob", vm((rws, 512), BF16)), ("dctx", vm((2, rws, 256), BF16)),
-        ("dqkv", vm((6, rws, 256), BF16)), ("yb", vm((caps * slots, 512), BF16)),
+        ("e", vm((rws, 512), F32)), ("dob", vm((rws, 512), BF16)),
+        ("dqkv", vm((6, rws, 256), BF16)),
         ("small", vm((8, 512), F32)), ("small_up", vm((8, 1, 256), F32)), ("small_qkv", vm((6, 1, 256), F32)),
         ("grads", vm((UNITS, 2, 512, 256), BF16)), ("cr", vm((UNITS, 2, 256, 256), BF16)), ("yr", vm((UNITS, 256, 256), BF16)),
-        ("xr", vm((UNITS, 128, 256), BF16)), ("zr", vm((UNITS, depth - 1, 128 // depth, 256), BF16)), ("f", vm((UNITS, 512, 256), BF16)),
+        ("xr", vm((UNITS, 128, 256), BF16)), ("zr", vm((UNITS, depth - 1, 128 // depth, 256), BF16)),
         ("sg", vm((1, 2, 128, 128), F32)), ("scr", vm((1, 2, 64, 128), F32)), ("syr", vm((1, 64, 128), F32)),
-        ("sxr", vm((1, 32, 128), F32)), ("szr", vm((1, depth - 1, 32 // depth, 128), F32)), ("sf", vm((1, 128, 128), F32)),
-        ("lsem", pltpu.SemaphoreType.DMA((20,))), ("osem", pltpu.SemaphoreType.DMA((UNITS + 3,))), ("bsem", pltpu.SemaphoreType.DMA((4,))),
+        ("sxr", vm((1, 32, 128), F32)), ("szr", vm((1, depth - 1, 32 // depth, 128), F32)),
+        ("lsem", pltpu.SemaphoreType.DMA((20,))), ("bsem", pltpu.SemaphoreType.DMA((4,))),
         ("wsend", pltpu.SemaphoreType.DMA((UNITS, 3))), ("wrecv", pltpu.SemaphoreType.DMA((UNITS, 3))),
         ("gsend", pltpu.SemaphoreType.DMA(sems)), ("grecv", pltpu.SemaphoreType.DMA(sems)),
     ]
     names = [n for n, _, _ in ins] + [n for n, _, _ in outs] + [n for n, _ in scr]
     y, dx, f, s = pl.pallas_call(
         functools.partial(kernel, caps, slots, pad, names),
-        out_shape=[jax.ShapeDtypeStruct(s, d) for _, s, d in outs],
+        out_shape=[vm(s, d) for _, s, d in outs],
         in_specs=[s for _, _, s in ins],
-        out_specs=[A] * len(outs),
+        out_specs=[V] * len(outs),
         scratch_shapes=[s for _, s in scr],
-        compiler_params=pltpu.CompilerParams(vmem_limit_bytes=61 << 20, collective_id=0, has_side_effects=True),
+        compiler_params=pltpu.CompilerParams(vmem_limit_bytes=VLIM, collective_id=0, has_side_effects=True),
         name="layer",
     )(*[v for _, v, _ in ins])
     results = [
@@ -721,15 +695,14 @@
     y, dx, qkv, out, up, down, qvb, ob, ub, db, gg, sh = pl.pallas_call(
         finish,
         out_shape=[jax.ShapeDtypeStruct(s, d) for s, d, _ in results],
-        in_specs=[A, V, A, A],
+        in_specs=[V, V, V, V],
         out_specs=[s for _, _, s in results],
         scratch_shapes=[
-            vm((UNITS, 512, 256), BF16), vm(y.shape, BF16), vm(dx.shape, F32), vm((UNITS, 512, 256), F32),
-            pltpu.SemaphoreType.DMA((UNITS,)), pltpu.SemaphoreType.DMA((2 * UNITS,)), pltpu.SemaphoreType.DMA((4,)),
+            vm((UNITS, 512, 256), F32), pltpu.SemaphoreType.DMA((2 * UNITS,)), pltpu.SemaphoreType.DMA((2,)),
         ],
-        compiler_params=pltpu.CompilerParams(vmem_limit_bytes=61 << 20),
+        compiler_params=pltpu.CompilerParams(vmem_limit_bytes=12 << 20),
         name="finish",
-    )(f, s, y, dx)
+    )(*[pltpu.with_memory_space_constraint(v, pltpu.VMEM) for v in (f, s, y, dx)])
     return y, dx, qkv, qvb, out, ob[0], up, ub[0], down, db[0], gg, sh
 
 

time: 95.3 us -> 91.1 us (0.956)
  Pallas kernels: 93.8 us -> 90.1 us
    pallas_call x1, Pallas kernels: 7.59 us -> 4.09 us  [shards(): pl.pallas_call(finish, out_shape=[jax.ShapeDtypeStruct(s, d) for s, d, _...]
where the time goes in v4:
time: 91.1 us; the launch traced here: 90.7 us
  Pallas kernels  90.1 us (99%)
    pallas_call x1, Pallas kernels, shards(): pl.pallas_call(functools.partial(kernel, caps, slots, pad, names), out_sh...  86 us
    pallas_call x1, Pallas kernels, shards(): pl.pallas_call(finish, out_shape=[jax.ShapeDtypeStruct(s, d) for s, d, _...  4.09 us

profile of v4, /device:TPU:0, one launch (start us, length us, event | category | flops | bytes accessed | tf_op | source)
XLA Modules:
  0.0 90.7 jit_solution(18384469436605347408)
XLA Ops:
  0.6 86.0 %layer.1 = (bf16[616,512]{1,0:T(8,128)(2,1)S(1)}, f32[616,512]{1,0:T(8,128)S(1)}, bf16[12,512,256]{2,1,0:T(8,128)(2,1)S(1)}, f32[1,128,128]{2,1,0:T(8,128)S(1)}) custom-call(bf16[1232,512]{1,0:T(8,128)(2,1)} %all_refs_0_.1, bf16[1232,512]{1,0:T(8,128)(2,1)} %all_refs_1_.1, s32[16]{0:T(128)} %all_refs_2_.1, bf16[3,512,256]{2,1,0:T(8,128)(2,1)} %all_refs_3_.1, ...), custom_call_target="tpu_custom_call" | custom-call | tf_op jit(solution)/shard_map/layer/pallas_call | solution.py:681
  86.6 4.1 %finish.1 = (bf16[616,512]{1,0:T(8,128)(2,1)}, f32[616,512]{1,0:T(8,128)}, f32[3,512,256]{2,1,0:T(8,128)}, f32[256,512]{1,0:T(8,128)}, f32[512,1024]{1,0:T(8,128...) custom-call(bf16[12,512,256]{2,1,0:T(8,128)(2,1)S(1)} %get-tuple-ele, ...), custom_call_target="tpu_custom_call" | custom-call | tf_op jit(solution)/shard_map/finish/pallas_call | solution.py:695

commit v5 on v4

--- a/solution.py
+++ b/solution.py
@@ -13,6 +13,8 @@
 BF16 = jnp.bfloat16
 LOG2E = 1.4426950408889634
 UNITS = 12
+BIG = 11
+FINAL = 14
 VLIM = 54 << 20
 MESH = pl.DeviceIdType.MESH
 
@@ -157,21 +159,26 @@
         self.dqkv[s * 3 + 1, r, :] = (self.unstack(nn(ds, q)) * HD**-0.5).astype(BF16)
         self.dqkv[s * 3, r, :] = (tn(ds, self.stack(k)) * HD**-0.5).astype(BF16)
 
+    def half_rows(self, i):
+        tile = self.rows // 4
+        return pl.ds(pl.multiple_of(i * tile, 16), tile)
+
+    def out_product(self, slot, r):
+        c = self.ctx[slot, r, :]
+        return jnp.concatenate([nn(c, self.w[slot * UNITS + 3, k * 256 : (k + 1) * 256, :]) for k in range(2)], axis=1)
+
+    def project_own(self, i):
+        r = self.half_rows(i)
+        self.h1[r, :] = self.xs[r, :].astype(F32) + self.out_product(0, r) + self.ob[...].astype(F32).reshape(1, -1)
+
     def project(self, i):
-        tile = self.rows // 4
-        r = pl.ds(pl.multiple_of(i * tile, 16), tile)
+        r = self.half_rows(i)
         gain, shift = self.gains[1:2, :].astype(F32), self.shifts[1:2, :].astype(F32)
-        c0, c1 = self.ctx[0, r, :], self.ctx[1, r, :]
-        halves = []
-        for n in range(2):
-            w = slice(n * 256, (n + 1) * 256)
-            halves.append(nn(c0, self.w[3, w, :]) + nn(c1, self.w[UNITS + 3, w, :]))
-        o = jnp.concatenate(halves, axis=1)
-        h1 = self.xs[r, :].astype(F32) + o + self.ob[...].astype(F32).reshape(1, -1)
+        h1 = self.h1[r, :] + self.out_product(1, r)
         self.h1[r, :] = h1
         n, inv = norm(h1)
         self.n2[r, :] = n
-        self.r2[r, :] = jnp.broadcast_to(inv, (tile, 128))
+        self.r2[r, :] = jnp.broadcast_to(inv, (n.shape[0], 128))
         self.a2[r, :] = (n * gain + shift).astype(BF16)
 
     def wup(self, m):
@@ -250,9 +257,13 @@
         self.ctx[s] = back.astype(BF16)
 
     def qkv_grad(self, i):
-        s, j = i // 3, lax.rem(i, 3)
+        s, j = i // 3, i % 3
         d = self.dqkv[i]
-        self.grads[9 + j, s] = tn(self.a1[...], d).astype(BF16)
+        w = tn(self.a1[...], d).astype(BF16)
+        if j < 2:
+            self.grads[9 + j, s] = w
+        else:
+            self.hg[0, s], self.hg[1, s] = w[:256], w[256:]
         self.small_qkv[i] = colsum(d.astype(F32))
 
     def first_grad(self, i):
@@ -309,9 +320,10 @@
         self.depth = depth
         self.to_z = [(lax.rem(self.z + k, depth) * 4 + lax.rem(dp, 4), t) for k in range(1, depth)]
         self.z_of = [lax.rem(self.z + k, depth) for k in range(1, depth)]
+        self.to_far = [(z * 4 + (1 - self.x) * 2 + self.core, t) for z in self.z_of]
 
     def all(self):
-        return [self.to_y, self.to_x, self.to_core] + self.to_z
+        return [self.to_y, self.to_x, self.to_core] + self.to_z + self.to_far
 
     def greet(self):
         barrier = pltpu.get_barrier_semaphore()
@@ -366,8 +378,9 @@
 
 
 class Reduce:
-    def __init__(self, peers, refs, sem0, send, recv):
+    def __init__(self, peers, refs, sem0, send, recv, wide=False):
         self.p = peers
+        self.wide = wide
         self.g, self.cr, self.yr, self.xr, self.zr, self.f = refs
         self.sem0, self.send, self.recv = sem0, send, recv
         self.count = self.g.shape[0]
@@ -378,8 +391,9 @@
     def sems(self, n, k):
         return self.send.at[self.sem0 + n, k], self.recv.at[self.sem0 + n, k]
 
-    def c(self, n):
-        return remote(self.g.at[n, :, rows(1 - self.p.core, self.half)], self.cr.at[n], *self.sems(n, 0), self.p.to_core)
+    def c(self, n, slot):
+        theirs = self.g.at[n, slot, rows(1 - self.p.core, self.half)]
+        return remote(theirs, self.cr.at[n, slot], *self.sems(n, (5 + 2 * self.p.depth - 2) if slot == 0 else 0), self.p.to_core)
 
     def y(self, n):
         return remote(self.cr.at[n, 1], self.yr.at[n], *self.sems(n, 1), self.p.to_y)
@@ -404,9 +418,12 @@
 
     def za(self, n):
         part = self.f.at[n, self.own_shard()]
-        return [
-            remote(part, part, *self.sems(n, 4 + self.p.depth + k), self.p.to_z[k]) for k in range(self.p.depth - 1)
-        ]
+        depth = self.p.depth
+        copies = [remote(part, part, *self.sems(n, 4 + depth + k), self.p.to_z[k]) for k in range(depth - 1)]
+        if self.wide:
+            copies.append(remote(part, part, *self.sems(n, 3), self.p.to_x))
+            copies += [remote(part, part, *self.sems(n, 4 + 2 * depth + k), self.p.to_far[k]) for k in range(depth - 1)]
+        return copies
 
     def xa(self, n):
         part = self.f.at[n, pl.ds(pl.multiple_of(self.p.core * self.half + self.p.x * self.quarter, self.quarter), self.quarter)]
@@ -417,16 +434,20 @@
         return remote(part, part, *self.sems(n, 4), self.p.to_core)
 
     def c_start(self, n):
-        self.c(n).start()
+        self.c(n, 1).start()
+
+    def c_start_own(self, n):
+        self.c(n, 0).start()
 
     def c_done(self, n):
-        self.c(n).wait_recv()
-        self.cr[n] = self.cr[n] + self.g[n, :, rows(self.p.core, self.half), :]
+        self.c(n, 1).wait_recv()
+        self.cr[n, 1] = self.cr[n, 1] + self.g[n, 1, rows(self.p.core, self.half), :]
         self.y(n).start()
 
     def y_done(self, n):
+        self.c(n, 0).wait_recv()
         self.y(n).wait_recv()
-        self.cr[n, 0] = self.cr[n, 0] + self.yr[n]
+        self.cr[n, 0] = self.cr[n, 0] + self.g[n, 0, rows(self.p.core, self.half), :] + self.yr[n]
         self.x(n).start()
 
     def x_done(self, n):
@@ -452,6 +473,11 @@
             copy.wait_recv()
         self.xa(n).start()
 
+    def xza_done(self, n):
+        for copy in self.za(n):
+            copy.wait_recv()
+        self.ca(n).start()
+
     def xa_done(self, n):
         self.xa(n).wait_recv()
         self.ca(n).start()
@@ -460,7 +486,8 @@
         self.ca(n).wait_recv()
 
     def drain(self, n):
-        for copy in [self.c(n), self.y(n), self.x(n), self.xa(n), self.ca(n)] + self.z(n) + self.za(n):
+        across = [] if self.wide else [self.xa(n)]
+        for copy in across + [self.c(n, 0), self.c(n, 1), self.y(n), self.x(n), self.ca(n)] + self.z(n) + self.za(n):
             copy.wait_send()
 
 
@@ -473,27 +500,34 @@
 
 
 ON_WEIGHTS = ("relay_x", "relay_c", "ready")
-ON_GRADS = ("c_start", "c_done", "y_done", "x_done", "z_done", "za_done", "xa_done", "ca_done")
+ON_GRADS = ("c_start", "c_done", "y_done", "x_done", "z_done", "za_done", "xa_done", "ca_done", "xza_done")
 PLAN = {
     "norm_one": (),
     "qkv_own": (),
     "att_own": ((1, 0, (0,)), ),
     "widen_g": ((0, 0, (1,)), ),
-    "qkv_other": ((0, 0, (2, 100, 3, 200,)), (1, 0, (101, 4, 201,)), (2, 0, (102, 5, 202,)), ),
-    "att_other": ((0, 0, (103,)), (1, 0, (104, 6,)), ),
-    "proj": ((0, 0, (105, 7, 8, 203,)), ),
-    "updown": ((0, 0, (9, 106,)), (0, 1, (204,)), (0, 3, (10,)), (1, 0, (1000, 107,)), (1, 1, (205,)), (1, 2, (11,)), (1, 3, (108, 1100,)), (2, 0, (1001,)), (2, 1, (206,)), (2, 2, (109,)), (2, 3, (1101,)), (3, 0, (1002,)), (3, 1, (110, 207,)), ),
-    "hbug": ((0, 0, (1003, 111, 1102,)), (0, 1, (1200, 208,)), (1, 0, (1004,)), (1, 1, (209,)), (1, 2, (1103,)), (1, 3, (1201,)), (2, 0, (1005, 1300,)), (2, 1, (210,)), (3, 0, (1006, 1202, 1104,)), (3, 1, (211,)), (3, 2, (1301,)), ),
-    "sg": ((0, 0, (1007, 1400,)), (1, 0, (1105, 1203,)), (2, 0, (1302,)), ),
-    "ntb": (),
-    "ob": ((0, 0, (1401, 1204, 1303, 1500, 1106,)), ),
-    "ab": ((0, 0, (1008,)), (1, 0, (1402, 1205, 1107,)), (2, 0, (1501, 1304,)), (3, 0, (1600, 1403, 1206, 1108,)), ),
-    "qg": ((0, 0, (1700, 1502, 1305,)), (1, 0, (1009, 1601, 1404, 1207,)), (2, 0, (1010, 1306, 1109, 1503,)), (2, 1, (1701,)), ),
-    "fg": ((0, 0, (1011,)), (1, 0, (1602, 1208, 1405, 1110,)), (3, 0, (1702, 1307,)), ),
-    "nob": ((0, 0, (1504,)), ),
-    "mo": ((0, 0, (1012, 1603,)), (1, 0, (1406, 1209, 1111,)), (2, 0, (1703, 1308,)), (3, 0, (1505,)), ),
-    "lo": (),
-    "tail": ((0, 0, (1604, 1112, 1407, 1210, 1704, 1309, 1506, 1605, 1408, 1211, 1705, 1212, 1310, 1507, 1606, 1409, 1706, 1311, 1508, 1312, 1607, 1410, 1707, 1509, 1608, 1411, 1708, 1412, 1510, 1609, 1709, 1511, 1512, 1610, 1710, 1611, 1612, 1711, 1712,)), ),
+    "pown": ((3, 0, (2,)), ),
+    "qkv_other": ((0, 0, (100, 3, 200,)), (1, 0, (101, 4, 201,)), (2, 0, (102, 5, 202,)), ),
+    "att_other": ((0, 0, (103,)), (1, 0, (104, 6, 7,)), ),
+    "proj": ((0, 0, (105, 8, 203,)), ),
+    "updown": ((0, 0, (204,)), (0, 1, (9,)), (0, 2, (1000, 106,)), (1, 0, (10, 205,)), (1, 1, (107, 1100,)), (1, 2, (1001, 11,)), (2, 0, (108, 206,)), (2, 1, (1101,)), (2, 2, (1002, 109,)), (3, 0, (207,)), (3, 1, (110,)), (3, 2, (1003, 1102, 1200,)), ),
+    "hbug": ((0, 0, (111, 208,)), (0, 2, (1004,)), (1, 0, (1201, 1103, 209,)), (1, 1, (1300,)), (1, 2, (1005,)), (2, 0, (210,)), (2, 1, (1202, 1104,)), (2, 2, (1006,)), (2, 3, (1301,)), (3, 0, (211,)), (3, 1, (1400,)), (3, 2, (1007, 1203, 1105,)), (3, 3, (1302,)), ),
+    "sg": ((2, 0, (1401,)), (3, 0, (1204, 1106,)), ),
+    "ntb": ((0, 0, (1500, 1303,)), ),
+    "ob1": ((0, 0, (1402, 1205, 1107,)), ),
+    "ob0": ((0, 0, (1008,)), ),
+    "ab": ((0, 0, (1501, 1304,)), (1, 0, (1600, 1403, 1206, 1108,)), (2, 0, (1700, 1502, 1305,)), (3, 0, (1601, 1404, 1207,)), ),
+    "qg3": ((0, 0, (1701, 1503, 1306,)), ),
+    "qg0": ((0, 0, (1009, 1602,)), ),
+    "qg4": ((0, 0, (1405, 1208,)), ),
+    "qg1": ((0, 0, (1010, 1109, 1702,)), ),
+    "qg5": ((0, 0, (1504, 1307,)), ),
+    "qg2": ((0, 0, (1011, 1012,)), ),
+    "fg": ((0, 0, (1603, 1110,)), (1, 0, (1406,)), (2, 0, (1703,)), (3, 0, (1308,)), ),
+    "nob": ((0, 0, (1505,)), ),
+    "mo": ((0, 0, (1013, 1604, 1209, 1111,)), (1, 0, (1407,)), (2, 0, (1704, 1112,)), (3, 0, (1506,)), ),
+    "lo": ((0, 0, (1605, 1210, 1113,)), ),
+    "tail": ((0, 0, (1408, 1705, 1309, 1211, 1507, 1606, 1212, 1706, 1213, 1310, 1508, 1311, 1409, 1607, 1312, 1707, 1313, 1410, 1608, 1411, 1708, 1509, 1412, 1413, 1510, 1609, 1811, 1709, 1711, 1812, 1610, 1813, 1712, 1710, 1713,)), ),
 }
 
 
@@ -504,17 +538,24 @@
     L.cap_base = peers.t * caps
     weights = Weights(peers, L.w, L.wsend, L.wrecv)
     big = Reduce(peers, (L.grads, L.cr, L.yr, L.xr, L.zr, L.f), 0, L.gsend, L.grecv)
-    small = Reduce(peers, (L.sg, L.scr, L.syr, L.sxr, L.szr, L.sf), UNITS, L.gsend, L.grecv)
+    half = Reduce(peers, (L.hg, L.hcr, L.hyr, L.hxr, L.hzr, L.hf), BIG, L.gsend, L.grecv, wide=True)
+    small = Reduce(peers, (L.sg, L.scr, L.syr, L.sxr, L.szr, L.sf), BIG + 2, L.gsend, L.grecv, wide=True)
+
+    def at(stage, unit):
+        if unit < BIG:
+            getattr(big, stage)(unit)
+        elif unit < BIG + 2:
+            getattr(half, stage)(unit - BIG)
+        else:
+            getattr(small, stage)(0)
 
     def arrive(codes):
         for code in codes:
             stage, unit = code // 100, code % 100
             if stage < 10:
                 getattr(weights, ON_WEIGHTS[stage])(unit)
-            elif unit == UNITS:
-                getattr(small, ON_GRADS[stage - 10])(0)
             else:
-                getattr(big, ON_GRADS[stage - 10])(unit)
+                at(ON_GRADS[stage - 10], unit)
 
     def run(name, count, *parts):
         def body(i):
@@ -536,20 +577,22 @@
         copy.start()
         local.append(copy)
 
-    load(L.tok, L.tok_v)
     for j in range(3):
         load(L.wqkv_a.at[j], L.w.at[j])
     for n in range(2):
         load(L.wo_a.at[:, pl.ds(n * 256, 256)], L.w.at[3, pl.ds(n * 256, 256)])
+    load(L.tok, L.tok_v)
     for n in range(4):
         load(L.wu_a.at[:, pl.ds(n * 256, 256)], L.w.at[4 + n])
     for n in range(4):
         for k in range(2):
             load(L.wd_a.at[pl.ds(n * 256, 256), pl.ds(k * 256, 256)], L.w.at[8 + n, pl.ds(k * 256, 256)])
     load(L.cot, L.cot_v)
-    local[0].wait()
+    for name in ("qvb", "ub", "ob", "db", "gains", "shifts", "lengths"):
+        load(getattr(L, name + "_h"), getattr(L, name))
+    local[5].wait()
     L.widen(L.tok_v, peers.t * caps * slots, L.xs)
-    for copy in local[1:]:
+    for copy in local[:5] + local[6:]:
         copy.wait()
     peers.meet()
     bias_send = [
@@ -574,63 +617,80 @@
     def output_rows():
         L.layer_out(L.stage, L.y_out)
 
+    def own(part, unit):
+        return lambda n: (part(n), big.c_start_own(unit + n))
+
     run("norm_one", 1, lambda i: (L.norm_one(), L.biases(0, L.qvb, L.ub)))
     run("qkv_own", 3, L.qkv)
     run("att_own", caps // 4, attend)
     run("widen_g", 1, lambda i: rows_and_biases())
+    run("pown", 4, L.project_own)
     run("qkv_other", 3, lambda j: L.qkv(3 + j))
     run("att_other", caps // 4, lambda i: attend(caps // 4 + i))
     run("proj", 4, L.project)
-    run("updown", 4, L.up, lambda n: L.up(4 + n), L.down_grad, lambda n: L.down_grad(4 + n))
-    run("hbug", 4, L.hidden_back, lambda n: L.hidden_back(4 + n), L.up_grad, lambda n: L.up_grad(4 + n))
+    run("updown", 4, lambda n: L.up(4 + n), lambda n: L.down_grad(4 + n), L.up, own(L.down_grad, 0))
+    run("hbug", 4, lambda n: L.hidden_back(4 + n), lambda n: L.up_grad(4 + n), L.hidden_back, own(L.up_grad, 4))
     run("sg", 4, L.second_grad)
     run("ntb", 1, lambda i: L.norm_two_back())
-    run("ob", 2, L.out_back)
+    run("ob1", 1, lambda i: L.out_back(1))
+    run("ob0", 1, lambda i: (L.out_back(0), big.c_start_own(8)))
     run("ab", caps // 2, lambda i: [L.attention_back(4 * i + k) for k in range(4)])
-    run("qg", 3, L.qkv_grad, lambda j: L.qkv_grad(3 + j))
+    for j in range(3):
+        run(f"qg{3 + j}", 1, lambda i: L.qkv_grad(3 + j))
+        run(f"qg{j}", 1, lambda i: L.qkv_grad(j))
+        for unit in (9 + j,) if j < 2 else (11, 12):
+            at("c_start_own", unit)
     run("fg", 4, L.first_grad)
-    run("nob", 1, lambda i: input_rows())
+    run("nob", 1, lambda i: (input_rows(), small.c_start_own(0)))
     run("mo", 4, L.mlp_out)
     run("lo", 1, lambda i: output_rows())
-    run("tail", 1, lambda i: None)
-
-    def drain(n):
-        weights.drain(n)
-        big.drain(n)
-
-    loop(UNITS, drain)
+    tail = PLAN["tail"][0][2]
+    arrive(tail[:-FINAL])
+    loop(UNITS, weights.drain)
+    loop(6, big.drain)
+    arrive(tail[-FINAL:])
+
+    loop(BIG - 6, lambda n: big.drain(6 + n))
+    loop(2, half.drain)
     small.drain(0)
 
 
-def finish(f, s, y, dx, y_out, dx_out, qkv, out, up, down, qvb, ob, ub, db, gg, sh, wide, sem_out, sem_io):
-    io = [pltpu.make_async_copy(y, y_out, sem_io.at[0]), pltpu.make_async_copy(dx, dx_out, sem_io.at[1])]
-    for copy in io:
+def finish(f, hf, s, y, dx, y_out, dx_out, qkv, out, up, down, qvb, ob, ub, db, gg, sh, wide, v1, v2, v3, v4, v5, v6, sem_out, sem_io):
+    io = []
+
+    def send(a, b, sem):
+        copy = pltpu.make_async_copy(a, b, sem)
         copy.start()
+        io.append(copy)
+
+    send(y, y_out, sem_io.at[0])
+    send(dx, dx_out, sem_io.at[1])
+
+    def row(first, count):
+        return jnp.concatenate([s[0, first + i : first + i + 1, :] for i in range(count)], axis=1)
+
     for n in range(UNITS):
-        wide[n] = f[n].astype(F32)
+        if n < BIG:
+            wide[n] = f[n].astype(F32)
+        else:
+            for k in range(2):
+                wide[n, k * 256 : (k + 1) * 256, :] = hf[k].astype(F32)
         if n < 4 or n == 8:
-            parts = []
             for k in range(2):
                 c = pl.ds(k * 256, 256)
-                dst = down.at[pl.ds(n * 256, 256), c] if n < 4 else out.at[:, c]
-                parts.append((wide.at[n, c], dst))
+                send(wide.at[n, c], down.at[pl.ds(n * 256, 256), c] if n < 4 else out.at[:, c], sem_out.at[2 * n + k])
         elif n < 8:
-            parts = [(wide.at[n], up.at[:, pl.ds((n - 4) * 256, 256)])]
+            send(wide.at[n], up.at[:, pl.ds((n - 4) * 256, 256)], sem_out.at[2 * n])
         else:
-            parts = [(wide.at[n], qkv.at[n - 9])]
-        for k, (a, b) in enumerate(parts):
-            copy = pltpu.make_async_copy(a, b, sem_out.at[2 * n + k])
-            copy.start()
-            io.append(copy)
-
-    def row(first, count):
-        return jnp.concatenate([s[0, first + i : first + i + 1, :] for i in range(count)], axis=1)
-
-    qvb[0:1, :], qvb[1:2, :] = row(0, 2), row(2, 2)
-    ub[...] = row(4, 8)
-    ob[...], db[...] = row(12, 4), row(16, 4)
-    gg[0:1, :], gg[1:2, :] = row(20, 4), row(24, 4)
-    sh[0:1, :], sh[1:2, :] = row(28, 4), row(32, 4)
+            send(wide.at[n], qkv.at[n - 9], sem_out.at[2 * n])
+        if n == 1:
+            v1[0:1, :], v1[1:2, :] = row(0, 2), row(2, 2)
+            v3[...] = row(4, 8)
+            v2[...], v4[...] = row(12, 4), row(16, 4)
+            v5[0:1, :], v5[1:2, :] = row(20, 4), row(24, 4)
+            v6[0:1, :], v6[1:2, :] = row(28, 4), row(32, 4)
+            for k, (a, b) in enumerate(((v1, qvb), (v2, ob), (v3, ub), (v4, db), (v5, gg), (v6, sh))):
+                send(a, b, sem_io.at[2 + k])
     for copy in io:
         copy.wait()
 
@@ -644,20 +704,21 @@
     rws = caps * pad
     V = pl.BlockSpec(memory_space=pltpu.VMEM)
     A = pl.BlockSpec(memory_space=pl.ANY)
-    S = pl.BlockSpec(memory_space=pltpu.SMEM)
     ins = [
-        ("tok", tokens, A), ("cot", cotangent, A), ("lengths", lengths, S),
+        ("tok", tokens, A), ("cot", cotangent, A), ("lengths_h", lengths, A),
         ("wqkv_a", qkv_weight, A), ("wo_a", out_weight, A), ("wu_a", up_weight, A), ("wd_a", down_weight, A),
-        ("qvb", qv_bias, V), ("ub", up_bias, V),
-        ("ob", out_bias, V), ("db", down_bias, V), ("gains", norm_gain, V), ("shifts", norm_shift, V),
+        ("qvb_h", qv_bias, A), ("ub_h", up_bias, A),
+        ("ob_h", out_bias, A), ("db_h", down_bias, A), ("gains_h", norm_gain, A), ("shifts_h", norm_shift, A),
     ]
     outs = [
         ("y_out", (caps * slots, 512), BF16), ("dx_out", (caps * slots, 512), F32),
-        ("f", (UNITS, 512, 256), BF16), ("sf", (1, 128, 128), F32),
+        ("f", (BIG, 512, 256), BF16), ("hf", (2, 256, 256), BF16), ("sf", (1, 128, 128), F32),
     ]
     vm = pltpu.VMEM
-    sems = UNITS + 1, 3 + 2 * depth
-    scr = [
+    sems = UNITS + 2, 3 + 3 * depth
+    held = [("qvb", qv_bias), ("ub", up_bias), ("ob", out_bias), ("db", down_bias), ("gains", norm_gain), ("shifts", norm_shift)]
+    scr = [(n, vm(v.shape, v.dtype)) for n, v in held] + [
+        ("lengths", pltpu.SMEM(lengths.shape, jnp.int32)),
         ("tok_v", vm((total, 512), BF16)), ("cot_v", vm((total, 512), BF16)),
         ("stage", vm((total + 16, 512), F32)), ("xs", vm((rws, 512), BF16)), ("g", vm((rws, 512), BF16)),
         ("n1", vm((rws, 512), F32)), ("r1", vm((rws, 128), F32)), ("a1", vm((rws, 512), BF16)),
@@ -669,16 +730,18 @@
         ("e", vm((rws, 512), F32)), ("dob", vm((rws, 512), BF16)),
         ("dqkv", vm((6, rws, 256), BF16)),
         ("small", vm((8, 512), F32)), ("small_up", vm((8, 1, 256), F32)), ("small_qkv", vm((6, 1, 256), F32)),
-        ("grads", vm((UNITS, 2, 512, 256), BF16)), ("cr", vm((UNITS, 2, 256, 256), BF16)), ("yr", vm((UNITS, 256, 256), BF16)),
-        ("xr", vm((UNITS, 128, 256), BF16)), ("zr", vm((UNITS, depth - 1, 128 // depth, 256), BF16)),
+        ("grads", vm((BIG, 2, 512, 256), BF16)), ("cr", vm((BIG, 2, 256, 256), BF16)), ("yr", vm((BIG, 256, 256), BF16)),
+        ("xr", vm((BIG, 128, 256), BF16)), ("zr", vm((BIG, depth - 1, 128 // depth, 256), BF16)),
+        ("hg", vm((2, 2, 256, 256), BF16)), ("hcr", vm((2, 2, 128, 256), BF16)), ("hyr", vm((2, 128, 256), BF16)),
+        ("hxr", vm((2, 64, 256), BF16)), ("hzr", vm((2, depth - 1, 64 // depth, 256), BF16)),
         ("sg", vm((1, 2, 128, 128), F32)), ("scr", vm((1, 2, 64, 128), F32)), ("syr", vm((1, 64, 128), F32)),
         ("sxr", vm((1, 32, 128), F32)), ("szr", vm((1, depth - 1, 32 // depth, 128), F32)),
-        ("lsem", pltpu.SemaphoreType.DMA((20,))), ("bsem", pltpu.SemaphoreType.DMA((4,))),
+        ("lsem", pltpu.SemaphoreType.DMA((28,))), ("bsem", pltpu.SemaphoreType.DMA((4,))),
         ("wsend", pltpu.SemaphoreType.DMA((UNITS, 3))), ("wrecv", pltpu.SemaphoreType.DMA((UNITS, 3))),
         ("gsend", pltpu.SemaphoreType.DMA(sems)), ("grecv", pltpu.SemaphoreType.DMA(sems)),
     ]
     names = [n for n, _, _ in ins] + [n for n, _, _ in outs] + [n for n, _ in scr]
-    y, dx, f, s = pl.pallas_call(
+    y, dx, f, hf, s = pl.pallas_call(
         functools.partial(kernel, caps, slots, pad, names),
         out_shape=[vm(s, d) for _, s, d in outs],
         in_specs=[s for _, _, s in ins],
@@ -690,19 +753,19 @@
     results = [
         (y.shape, BF16, A), (dx.shape, F32, A), (qkv_weight.shape, F32, A), (out_weight.shape, F32, A),
         (up_weight.shape, F32, A), (down_weight.shape, F32, A),
-        (qv_bias.shape, F32, V), ((1, 512), F32, V), ((1, up_bias.shape[0]), F32, V), ((1, 512), F32, V), ((2, 512), F32, V), ((2, 512), F32, V),
+        (qv_bias.shape, F32, A), ((1, 512), F32, A), ((1, up_bias.shape[0]), F32, A), ((1, 512), F32, A), ((2, 512), F32, A), ((2, 512), F32, A),
     ]
     y, dx, qkv, out, up, down, qvb, ob, ub, db, gg, sh = pl.pallas_call(
         finish,
         out_shape=[jax.ShapeDtypeStruct(s, d) for s, d, _ in results],
-        in_specs=[V, V, V, V],
+        in_specs=[V] * 5,
         out_specs=[s for _, _, s in results],
         scratch_shapes=[
-            vm((UNITS, 512, 256), F32), pltpu.SemaphoreType.DMA((2 * UNITS,)), pltpu.SemaphoreType.DMA((2,)),
+            vm((UNITS, 512, 256), F32), *[vm(s, F32) for s, _, _ in results[6:]], pltpu.SemaphoreType.DMA((2 * UNITS,)), pltpu.SemaphoreType.DMA((8,)),
         ],
         compiler_params=pltpu.CompilerParams(vmem_limit_bytes=12 << 20),
         name="finish",
-    )(*[pltpu.with_memory_space_constraint(v, pltpu.VMEM) for v in (f, s, y, dx)])
+    )(*[pltpu.with_memory_space_constraint(v, pltpu.VMEM) for v in (f, hf, s, y, dx)])
     return y, dx, qkv, qvb, out, ob[0], up, ub[0], down, db[0], gg, sh
 
 

time: 91.1 us -> 90 us (0.988)
  Pallas kernels: 90.1 us -> 89 us
where the time goes in v5:
time: 90 us; the launch traced here: 89.8 us
  Pallas kernels  89 us (99%)
    pallas_call x1, Pallas kernels, shards(): pl.pallas_call(functools.partial(kernel, caps, slots, pad, names), out_sh...  85.4 us
    pallas_call x1, Pallas kernels, shards(): pl.pallas_call(finish, out_shape=[jax.ShapeDtypeStruct(s, d) for s, d, _...  3.57 us

profile of v5, /device:TPU:0, one launch (start us, length us, event | category | flops | bytes accessed | tf_op | source)
XLA Modules:
  0.0 89.8 jit_solution(7953697100892897152)
XLA Ops:
  0.6 85.4 %layer.1 = (bf16[616,512]{1,0:T(8,128)(2,1)S(1)}, f32[616,512]{1,0:T(8,128)S(1)}, bf16[11,512,256]{2,1,0:T(8,128)(2,1)S(1)}, bf16[2,256,256]{2,1,0:T(8,128)(2,1)S(1)}, f32[1,128,128]{2,1,0:T(8,128)S(1)}) custom-call(bf16[1232,512]{1,0:T(8,128)(2,1)} %all_refs_0_.1, bf16[1232,512]{1,0:T(8,128)(2,1)} %all_refs_1_.1, s32[16]{0:T(128)} %all_refs_2_.1, ...), custom_call_target="tpu_custom_call" | custom-call | tf_op jit(solution)/shard_map/layer/pallas_call | solution.py:744
  86.1 3.6 %finish.1 = (bf16[616,512]{1,0:T(8,128)(2,1)}, f32[616,512]{1,0:T(8,128)}, f32[3,512,256]{2,1,0:T(8,128)}, f32[256,512]{1,0:T(8,128)}, f32[512,1024]{1,0:T(8,128...) custom-call(bf16[11,512,256]{2,1,0:T(8,128)(2,1)S(1)} %get-tuple-ele, ...), custom_call_target="tpu_custom_call" | custom-call | tf_op jit(solution)/shard_map/finish/pallas_call | solution.py:758

commit v6 on v5

--- a/solution.py
+++ b/solution.py
@@ -123,44 +123,35 @@
     def attention(self, i):
         s, c = i // self.caps, lax.rem(i, self.caps)
         r = self.crows(c)
-        q = self.pqkv[s * 3, r, :]
-        km = self.stack(self.pqkv[s * 3 + 1, r, :])
-        vm = self.stack(self.pqkv[s * 3 + 2, r, :])
-        st = nt(km, q)
+        scores = nt(self.stack(self.pqkv[s * 3, r, :]), self.pqkv[s * 3 + 1, r, :])
         length = self.lengths[self.cap_base + c]
-        jj = lax.broadcasted_iota(jnp.int32, (self.pad, self.pad), 0)
-        ii = lax.broadcasted_iota(jnp.int32, (self.pad, self.pad), 1)
+        ii = lax.broadcasted_iota(jnp.int32, (self.pad, self.pad), 0)
+        jj = lax.broadcasted_iota(jnp.int32, (self.pad, self.pad), 1)
         allowed = (jj <= ii) & (jj < length)
         blocks = []
         for h in range(4):
-            blk = jnp.where(allowed, st[h * self.pad : (h + 1) * self.pad], -1e30)
-            top = jnp.max(blk, axis=0, keepdims=True)
+            blk = jnp.where(allowed, scores[h * self.pad : (h + 1) * self.pad], -1e30)
+            top = jnp.max(blk, axis=1, keepdims=True)
             e = jnp.exp2((blk - top) * (HD**-0.5 * LOG2E))
-            blocks.append(e * (1.0 / jnp.sum(e, axis=0, keepdims=True)))
+            blocks.append(e * (1.0 / jnp.sum(e, axis=1, keepdims=True)))
         p = jnp.concatenate(blocks, axis=0)
         self.probs[i] = p
-        self.ctx[s, r, :] = tn(p.astype(BF16), vm).astype(BF16)
+        self.ctx[s, r, :] = self.unstack(nn(p.astype(BF16), self.pqkv[s * 3 + 2, r, :])).astype(BF16)
 
     def attention_back(self, i):
         s, c = i // self.caps, lax.rem(i, self.caps)
         r = self.crows(c)
-        q = self.pqkv[s * 3, r, :]
-        k = self.pqkv[s * 3 + 1, r, :]
-        v = self.pqkv[s * 3 + 2, r, :]
-        d = self.ctx[s, r, :]
+        q = self.stack(self.pqkv[s * 3, r, :])
+        d = self.stack(self.ctx[s, r, :])
         p = self.probs[i]
-        self.dqkv[s * 3 + 2, r, :] = self.unstack(nn(p.astype(BF16), d)).astype(BF16)
-        dp = nt(self.stack(v), d)
-        blocks = []
-        for h in range(4):
-            rr = slice(h * self.pad, (h + 1) * self.pad)
-            blocks.append(p[rr] * (dp[rr] - jnp.sum(dp[rr] * p[rr], axis=0, keepdims=True)))
-        ds = jnp.concatenate(blocks, axis=0).astype(BF16)
-        self.dqkv[s * 3 + 1, r, :] = (self.unstack(nn(ds, q)) * HD**-0.5).astype(BF16)
-        self.dqkv[s * 3, r, :] = (tn(ds, self.stack(k)) * HD**-0.5).astype(BF16)
+        self.dqkv[s * 3 + 2, r, :] = tn(p.astype(BF16), d).astype(BF16)
+        dp = nt(d, self.pqkv[s * 3 + 2, r, :])
+        ds = (p * (dp - jnp.sum(dp * p, axis=1, keepdims=True))).astype(BF16)
+        self.dqkv[s * 3 + 1, r, :] = (tn(ds, q) * HD**-0.5).astype(BF16)
+        self.dqkv[s * 3, r, :] = (self.unstack(nn(ds, self.pqkv[s * 3 + 1, r, :])) * HD**-0.5).astype(BF16)
 
     def half_rows(self, i):
-        tile = self.rows // 4
+        tile = self.rows // 2
         return pl.ds(pl.multiple_of(i * tile, 16), tile)
 
     def out_product(self, slot, r):
@@ -506,27 +497,27 @@
     "qkv_own": (),
     "att_own": ((1, 0, (0,)), ),
     "widen_g": ((0, 0, (1,)), ),
-    "pown": ((3, 0, (2,)), ),
-    "qkv_other": ((0, 0, (100, 3, 200,)), (1, 0, (101, 4, 201,)), (2, 0, (102, 5, 202,)), ),
+    "pown": (),
+    "qkv_other": ((0, 0, (2, 100, 3, 200,)), (1, 0, (101, 4, 201,)), (2, 0, (102, 5, 202,)), ),
     "att_other": ((0, 0, (103,)), (1, 0, (104, 6, 7,)), ),
     "proj": ((0, 0, (105, 8, 203,)), ),
-    "updown": ((0, 0, (204,)), (0, 1, (9,)), (0, 2, (1000, 106,)), (1, 0, (10, 205,)), (1, 1, (107, 1100,)), (1, 2, (1001, 11,)), (2, 0, (108, 206,)), (2, 1, (1101,)), (2, 2, (1002, 109,)), (3, 0, (207,)), (3, 1, (110,)), (3, 2, (1003, 1102, 1200,)), ),
-    "hbug": ((0, 0, (111, 208,)), (0, 2, (1004,)), (1, 0, (1201, 1103, 209,)), (1, 1, (1300,)), (1, 2, (1005,)), (2, 0, (210,)), (2, 1, (1202, 1104,)), (2, 2, (1006,)), (2, 3, (1301,)), (3, 0, (211,)), (3, 1, (1400,)), (3, 2, (1007, 1203, 1105,)), (3, 3, (1302,)), ),
-    "sg": ((2, 0, (1401,)), (3, 0, (1204, 1106,)), ),
-    "ntb": ((0, 0, (1500, 1303,)), ),
-    "ob1": ((0, 0, (1402, 1205, 1107,)), ),
+    "updown": ((0, 0, (204,)), (0, 1, (9,)), (0, 2, (1000, 106,)), (1, 0, (10, 205,)), (1, 1, (107, 1100,)), (1, 2, (1001,)), (1, 3, (11,)), (2, 0, (108, 206,)), (2, 1, (1101,)), (2, 2, (1002,)), (2, 3, (109,)), (3, 0, (207,)), (3, 1, (1102, 110,)), (3, 2, (1003, 1200,)), ),
+    "hbug": ((0, 0, (111, 208,)), (0, 1, (1103,)), (0, 2, (1004,)), (1, 0, (1201, 209,)), (1, 1, (1300,)), (1, 2, (1005, 1104,)), (2, 0, (210,)), (2, 1, (1202,)), (2, 2, (1006,)), (2, 3, (1301, 1105,)), (3, 0, (211,)), (3, 1, (1400,)), (3, 2, (1007, 1203,)), ),
+    "sg": ((0, 0, (1302, 1106,)), (2, 0, (1401,)), (3, 0, (1204,)), ),
+    "ntb": ((0, 0, (1500, 1303, 1107,)), ),
+    "ob1": ((0, 0, (1402, 1205,)), ),
     "ob0": ((0, 0, (1008,)), ),
     "ab": ((0, 0, (1501, 1304,)), (1, 0, (1600, 1403, 1206, 1108,)), (2, 0, (1700, 1502, 1305,)), (3, 0, (1601, 1404, 1207,)), ),
     "qg3": ((0, 0, (1701, 1503, 1306,)), ),
-    "qg0": ((0, 0, (1009, 1602,)), ),
-    "qg4": ((0, 0, (1405, 1208,)), ),
-    "qg1": ((0, 0, (1010, 1109, 1702,)), ),
-    "qg5": ((0, 0, (1504, 1307,)), ),
-    "qg2": ((0, 0, (1011, 1012,)), ),
-    "fg": ((0, 0, (1603, 1110,)), (1, 0, (1406,)), (2, 0, (1703,)), (3, 0, (1308,)), ),
+    "qg0": ((0, 0, (1009,)), ),
+    "qg4": ((0, 0, (1602, 1405, 1208,)), ),
+    "qg1": ((0, 0, (1010, 1109,)), ),
+    "qg5": ((0, 0, (1702, 1504, 1307,)), ),
+    "qg2": ((0, 0, (1011, 1012, 1110,)), ),
+    "fg": ((0, 0, (1603,)), (1, 0, (1406,)), (2, 0, (1111, 1703,)), (3, 0, (1308,)), ),
     "nob": ((0, 0, (1505,)), ),
-    "mo": ((0, 0, (1013, 1604, 1209, 1111,)), (1, 0, (1407,)), (2, 0, (1704, 1112,)), (3, 0, (1506,)), ),
-    "lo": ((0, 0, (1605, 1210, 1113,)), ),
+    "mo": ((0, 0, (1013, 1604, 1209, 1112, 1407,)), (2, 0, (1704, 1113,)), (3, 0, (1506,)), ),
+    "lo": ((0, 0, (1605, 1210,)), ),
     "tail": ((0, 0, (1408, 1705, 1309, 1211, 1507, 1606, 1212, 1706, 1213, 1310, 1508, 1311, 1409, 1607, 1312, 1707, 1313, 1410, 1608, 1411, 1708, 1509, 1412, 1413, 1510, 1609, 1811, 1709, 1711, 1812, 1610, 1813, 1712, 1710, 1713,)), ),
 }
 
@@ -624,10 +615,10 @@
     run("qkv_own", 3, L.qkv)
     run("att_own", caps // 4, attend)
     run("widen_g", 1, lambda i: rows_and_biases())
-    run("pown", 4, L.project_own)
+    run("pown", 2, L.project_own)
     run("qkv_other", 3, lambda j: L.qkv(3 + j))
     run("att_other", caps // 4, lambda i: attend(caps // 4 + i))
-    run("proj", 4, L.project)
+    run("proj", 2, L.project)
     run("updown", 4, lambda n: L.up(4 + n), lambda n: L.down_grad(4 + n), L.up, own(L.down_grad, 0))
     run("hbug", 4, lambda n: L.hidden_back(4 + n), lambda n: L.up_grad(4 + n), L.hidden_back, own(L.up_grad, 4))
     run("sg", 4, L.second_grad)

time: 90 us -> 89 us (0.989)
  Pallas kernels: 89 us -> 87.9 us
    pallas_call x1, Pallas kernels: 85.4 us -> 84.4 us  [shards(): pl.pallas_call(functools.partial(kernel, caps, slots, pad, names), out_sh...]
where the time goes in v6:
time: 89 us; the launch traced here: 88.8 us
  Pallas kernels  87.9 us (99%)
    pallas_call x1, Pallas kernels, shards(): pl.pallas_call(functools.partial(kernel, caps, slots, pad, names), out_sh...  84.4 us
    pallas_call x1, Pallas kernels, shards(): pl.pallas_call(finish, out_shape=[jax.ShapeDtypeStruct(s, d) for s, d, _...  3.57 us

profile of v6, /device:TPU:0, one launch (start us, length us, event | category | flops | bytes accessed | tf_op | source)
XLA Modules:
  0.0 88.8 jit_solution(11242802764245632922)
XLA Ops:
  0.6 84.4 %layer.1 = (bf16[616,512]{1,0:T(8,128)(2,1)S(1)}, f32[616,512]{1,0:T(8,128)S(1)}, bf16[11,512,256]{2,1,0:T(8,128)(2,1)S(1)}, bf16[2,256,256]{2,1,0:T(8,128)(2,1)S(1)}, f32[1,128,128]{2,1,0:T(8,128)S(1)}) custom-call(bf16[1232,512]{1,0:T(8,128)(2,1)} %all_refs_0_.1, bf16[1232,512]{1,0:T(8,128)(2,1)} %all_refs_1_.1, s32[16]{0:T(128)} %all_refs_2_.1, ...), custom_call_target="tpu_custom_call" | custom-call | tf_op jit(solution)/shard_map/layer/pallas_call | solution.py:735
  85.0 3.6 %finish.1 = (bf16[616,512]{1,0:T(8,128)(2,1)}, f32[616,512]{1,0:T(8,128)}, f32[3,512,256]{2,1,0:T(8,128)}, f32[256,512]{1,0:T(8,128)}, f32[512,1024]{1,0:T(8,128...) custom-call(bf16[11,512,256]{2,1,0:T(8,128)(2,1)S(1)} %get-tuple-ele, ...), custom_call_target="tpu_custom_call" | custom-call | tf_op jit(solution)/shard_map/finish/pallas_call | solution.py:749

commit v7 on v6

--- a/solution.py
+++ b/solution.py
@@ -14,7 +14,7 @@
 LOG2E = 1.4426950408889634
 UNITS = 12
 BIG = 11
-FINAL = 14
+FINAL = 9
 VLIM = 54 << 20
 MESH = pl.DeviceIdType.MESH
 
@@ -581,9 +581,7 @@
     load(L.cot, L.cot_v)
     for name in ("qvb", "ub", "ob", "db", "gains", "shifts", "lengths"):
         load(getattr(L, name + "_h"), getattr(L, name))
-    local[5].wait()
-    L.widen(L.tok_v, peers.t * caps * slots, L.xs)
-    for copy in local[:5] + local[6:]:
+    for copy in local[:5] + local[6:18] + local[19:21]:
         copy.wait()
     peers.meet()
     bias_send = [
@@ -593,6 +591,10 @@
     for copy in bias_send:
         copy.start()
     loop(UNITS, lambda u: weights.y(u).start())
+    local[5].wait()
+    L.widen(L.tok_v, peers.t * caps * slots, L.xs)
+    for copy in local[18:19] + local[21:]:
+        copy.wait()
     attend = lambda i: [L.attention(4 * i + k) for k in range(4)]
 
     def rows_and_biases():
@@ -638,10 +640,10 @@
     tail = PLAN["tail"][0][2]
     arrive(tail[:-FINAL])
     loop(UNITS, weights.drain)
-    loop(6, big.drain)
+    loop(9, big.drain)
     arrive(tail[-FINAL:])
 
-    loop(BIG - 6, lambda n: big.drain(6 + n))
+    loop(BIG - 9, lambda n: big.drain(9 + n))
     loop(2, half.drain)
     small.drain(0)
 

time: 89 us -> 89 us (level)
  no operation moved by 1% of the time
where the time goes in v7:
time: 89 us; the launch traced here: 88.9 us
  Pallas kernels  88 us (99%)
    pallas_call x1, Pallas kernels, shards(): pl.pallas_call(functools.partial(kernel, caps, slots, pad, names), out_sh...  84.5 us
    pallas_call x1, Pallas kernels, shards(): pl.pallas_call(finish, out_shape=[jax.ShapeDtypeStruct(s, d) for s, d, _...  3.57 us

profile of v7, /device:TPU:0, one launch (start us, length us, event | category | flops | bytes accessed | tf_op | source)
XLA Modules:
  0.0 88.9 jit_solution(16527788418708123975)
XLA Ops:
  0.6 84.5 %layer.1 = (bf16[616,512]{1,0:T(8,128)(2,1)S(1)}, f32[616,512]{1,0:T(8,128)S(1)}, bf16[11,512,256]{2,1,0:T(8,128)(2,1)S(1)}, bf16[2,256,256]{2,1,0:T(8,128)(2,1)S(1)}, f32[1,128,128]{2,1,0:T(8,128)S(1)}) custom-call(bf16[1232,512]{1,0:T(8,128)(2,1)} %all_refs_0_.1, bf16[1232,512]{1,0:T(8,128)(2,1)} %all_refs_1_.1, s32[16]{0:T(128)} %all_refs_2_.1, ...), custom_call_target="tpu_custom_call" | custom-call | tf_op jit(solution)/shard_map/layer/pallas_call | solution.py:737
  85.1 3.6 %finish.1 = (bf16[616,512]{1,0:T(8,128)(2,1)}, f32[616,512]{1,0:T(8,128)}, f32[3,512,256]{2,1,0:T(8,128)}, f32[256,512]{1,0:T(8,128)}, f32[512,1024]{1,0:T(8,128...) custom-call(bf16[11,512,256]{2,1,0:T(8,128)(2,1)S(1)} %get-tuple-ele, ...), custom_call_target="tpu_custom_call" | custom-call | tf_op jit(solution)/shard_map/finish/pallas_call | solution.py:751
